TPU v7x, 256 devices: a whole 4x4x8 slice. The times are simulated.
256 devices in a mesh: gz: 4 (over x), grid: 64 (over y, z, core).
Axes of the slice: x: 4, y: 4, z: 8, core: 2. Of those that a mesh axis runs over, the one named last changes fastest.
Arguments:
- rhs: bfloat16 [6, 128, 32, 128], P(None, 'grid'), may hold values from -6 to 6
- lower_updates: bfloat16 [4, 6, 128, 32, 128], P('gz', None, 'grid'), may hold values from -6 to 6
- diag_inv: bfloat16 [6, 128, 128, 128], P(None, 'grid'), may hold values from -0.5 to 0.5
- lower_blocks: bfloat16 [5, 128, 128, 128], P(None, 'grid'), may hold values from -0.5 to 0.5
- upper_inv: bfloat16 [6, 128, 128, 128], P(None, 'grid'), may hold values from -0.5 to 0.5
- upper_blocks: bfloat16 [5, 128, 128, 128], P(None, 'grid'), may hold values from -0.5 to 0.5
- parent: int32 [5, 128], P(None, 'grid'), may hold values from 0 to 127, as said below
- live_count: int32 [6, 64], P(None, 'grid'), may hold values from 1 to 2
Outputs:
- solution: bfloat16 [6, 128, 32, 128], P(None, 'grid')
Inputs may be any that keep to these rules, and one draw needn't show every extreme that they name: At level l the slots form aligned groups of S = min(128, 4 * 2 * 2 ** l) slots (those of min(64, 4 * 2 ** l) grid indices in a row); parent[l, g] lies in the group of g, between (g // S) * S and (g // S) * S + S - 1, and both ends are named in every group.
All inputs are finite; a program needn't handle non-finite values.
Results may differ from a plain program's by a relative error of at most 0.03.
Values may be sent and summed in bfloat16 or wider, within the bound.
A program may use at most 64 MiB of HBM per device.

v0:
```python
import jax
import jax.numpy as jnp
from jax import lax
from jax.sharding import PartitionSpec as P


def on_device(
    rhs, lower_updates, diag_inv, lower_blocks, upper_inv, upper_blocks, parent, live_count
):
    f32 = jnp.float32
    bf16 = jnp.bfloat16
    levels, slots, rows, width = rhs.shape
    own_slots = lax.axis_index("grid") * slots + jnp.arange(slots, dtype=jnp.int32)
    live = (jnp.arange(slots, dtype=jnp.int32)[None, :] < live_count).astype(f32)
    updates = lax.psum(lower_updates[0].astype(f32).astype(jnp.bfloat16), "gz").astype(jnp.float32)
    flat = rows * width
    incoming = jnp.zeros((slots, rows, width), f32)
    forward_all = []
    for level in range(levels):
        residual = (rhs[level].astype(f32) - updates[level] - incoming).astype(bf16)
        forward = jnp.einsum("srw,swv->srv", residual, diag_inv[level], preferred_element_type=f32)
        forward = (forward * live[level][:, None, None]).astype(bf16)
        forward_all.append(forward)
        if level + 1 < levels:
            sent = jnp.einsum(
                "srw,swv->srv", forward, lower_blocks[level], preferred_element_type=f32
            )
            sent = sent.astype(bf16).reshape(slots, flat)
            targets = parent[level]
            values = lax.all_gather(sent, "grid", axis=0, tiled=True)
            owners = lax.all_gather(targets, "grid", axis=0, tiled=True)
            onehot = (owners[None, :] == own_slots[:, None]).astype(bf16)
            summed = jnp.dot(onehot, values, preferred_element_type=f32)
            incoming = summed.reshape(slots, rows, width)
    answer = [None] * levels
    upper_flat = None
    for level in range(levels - 1, -1, -1):
        if level == levels - 1:
            target = forward_all[level].astype(f32)
        else:
            targets = parent[level]

            def select_parent(total, piece, first, targets=targets):
                wanted = jnp.arange(piece.shape[0], dtype=jnp.int32)
                chosen = (targets[:, None] == wanted[None, :]).astype(bf16)
                return jnp.dot(chosen, piece, preferred_element_type=f32)

            above = select_parent(
                jnp.zeros((slots, flat), f32),
                lax.all_gather(upper_flat, "grid", axis=0, tiled=True),
                jnp.int32(0),
            )
            above = above.astype(bf16).reshape(slots, rows, width)
            target = forward_all[level].astype(f32) - jnp.einsum(
                "srw,swv->srv", above, upper_blocks[level], preferred_element_type=f32
            )
        target = target.astype(bf16)
        result = jnp.einsum("srw,swv->srv", target, upper_inv[level], preferred_element_type=f32)
        solved = (result * live[level][:, None, None]).astype(bf16)
        answer[level] = solved
        upper_flat = solved.reshape(slots, flat)
    stacked = jnp.stack(answer)
    return stacked


def solution(mesh):
    return jax.shard_map(
        on_device,
        mesh=mesh,
        in_specs=(
            P(None, "grid", None, None),
            P("gz", None, "grid", None, None),
            P(None, "grid", None, None),
            P(None, "grid", None, None),
            P(None, "grid", None, None),
            P(None, "grid", None, None),
            P(None, "grid"),
            P(None, "grid"),
        ),
        out_specs=P(None, "grid", None, None),
        check_vma=False,
    )
```

profile of v0, /device:TPU:1, one launch (start us, length us, event | category | flops | bytes accessed | tf_op | source)
XLA Modules:
  0.0 849.4 jit_solution(444018859633957401)
XLA Ops:
  6.5 0.7 all-reduce.8.cloned.1.call-update
  7.3 0.7 fusion.132
  8.0 49.8 %all-reduce.8.cloned.1.call-done = bf16[6,2,32,128]{3,2,1,0:T(8,128)(2,1)} async-done(((bf16[6,2,32,128]{3,2,1,0:T(8,128)(2,1)}), bf16[6,2,32,128]{3,2,1,0:T(8,128)(2,1)}) %all-reduce.8.cloned.1.call-update) | async-done | bytes 98320 | tf_op jit(solution)/shard_map/psum | solution.py:15
  57.8 0.9 convert_element_type.162
  58.7 0.8 fusion
  59.5 1.0 convolution_convert_fusion.9
  60.5 0.6 reshape.133
  61.3 0.7 copy-done.7
  61.9 0.6 dynamic-slice
  64.5 19.4 %all-reduce.5 = (s32[128]{0:T(128)S(1)}, s32[128]{0:T(128)S(1)}, s32[128]{0:T(128)S(1)}, s32[128]{0:T(128)S(1)}, s32[128]{0:T(128)S(1)}) all-reduce(s32[128]{0:T(128)S(1)} %dynamic-update-slice, s32[128]{0:T(128)S(1)} %dynamic-update-slice.1, s32[128]{0:T(128)S(1)} %dynamic-update-slice.2, ...), channel_id=2, replica_groups=mesh['gz'=4,'grid'=64] {'grid'}, use_global_device_ids=true, to_apply=%add | all-reduce | flops 640 | bytes 5120
  83.9 57.2 %all-gather.26.cloned.1.call-done = bf16[64,2,4096]{2,1,0:T(2,128)(2,1)} async-done(((bf16[1,2,4096]{2,1,0:T(2,128)(2,1)}), bf16[64,2,4096]{2,1,0:T(2,128)(2,1)}) %all-gather.26.cloned.1.call-update) | async-done | bytes 1048592 | tf_op jit(solution)/shard_map/all_gather | solution.py:30
  141.1 1.5 reshape.134
  142.9 0.6 copy-done.2
  143.7 0.6 reshape.135
  144.4 74.7 %all-gather.28.cloned.1.call-done = bf16[64,2,4096]{2,1,0:T(2,128)(2,1)} async-done(((bf16[1,2,4096]{2,1,0:T(2,128)(2,1)}), bf16[64,2,4096]{2,1,0:T(2,128)(2,1)}) %all-gather.28.cloned.1.call-update) | async-done | bytes 1048592 | tf_op jit(solution)/shard_map/all_gather | solution.py:30
  219.1 1.5 reshape.136
  221.1 0.6 reshape.137
  221.8 74.7 %all-gather.30.cloned.1.call-done = bf16[64,2,4096]{2,1,0:T(2,128)(2,1)} async-done(((bf16[1,2,4096]{2,1,0:T(2,128)(2,1)}), bf16[64,2,4096]{2,1,0:T(2,128)(2,1)}) %all-gather.30.cloned.1.call-update) | async-done | bytes 1048592 | tf_op jit(solution)/shard_map/all_gather | solution.py:30
  296.5 1.5 reshape.138
  298.5 0.6 reshape.139
  299.2 74.7 %all-gather.32.cloned.1.call-done = bf16[64,2,4096]{2,1,0:T(2,128)(2,1)} async-done(((bf16[1,2,4096]{2,1,0:T(2,128)(2,1)}), bf16[64,2,4096]{2,1,0:T(2,128)(2,1)}) %all-gather.32.cloned.1.call-update) | async-done | bytes 1048592 | tf_op jit(solution)/shard_map/all_gather | solution.py:30
  373.9 1.5 reshape.140
  375.9 0.6 reshape.141
  376.6 74.7 %all-gather.34.cloned.1.call-done = bf16[64,2,4096]{2,1,0:T(2,128)(2,1)} async-done(((bf16[1,2,4096]{2,1,0:T(2,128)(2,1)}), bf16[64,2,4096]{2,1,0:T(2,128)(2,1)}) %all-gather.34.cloned.1.call-update) | async-done | bytes 1048592 | tf_op jit(solution)/shard_map/all_gather | solution.py:30
  451.3 1.5 reshape.142
  453.1 0.7 copy-done.4
  454.0 0.7 reshape.143
  454.7 74.7 %all-gather.36.cloned.1.call-done = bf16[64,2,4096]{2,1,0:T(2,128)(2,1)} async-done(((bf16[1,2,4096]{2,1,0:T(2,128)(2,1)}), bf16[64,2,4096]{2,1,0:T(2,128)(2,1)}) %all-gather.36.cloned.1.call-update) | async-done | bytes 1048592 | tf_op jit(solution)/shard_map/all_gather | solution.py:50
  529.4 1.5 reshape.144
  530.8 0.3 fusion.19
  531.1 0.7 copy-done.5
  532.0 0.7 reshape.145
  532.8 74.7 %all-gather.38.cloned.1.call-done = bf16[64,2,4096]{2,1,0:T(2,128)(2,1)} async-done(((bf16[1,2,4096]{2,1,0:T(2,128)(2,1)}), bf16[64,2,4096]{2,1,0:T(2,128)(2,1)}) %all-gather.38.cloned.1.call-update) | async-done | bytes 1048592 | tf_op jit(solution)/shard_map/all_gather | solution.py:50
  607.4 1.5 reshape.146
  608.9 0.3 fusion.20
  609.4 0.7 reshape.147
  610.1 74.7 %all-gather.40.cloned.1.call-done = bf16[64,2,4096]{2,1,0:T(2,128)(2,1)} async-done(((bf16[1,2,4096]{2,1,0:T(2,128)(2,1)}), bf16[64,2,4096]{2,1,0:T(2,128)(2,1)}) %all-gather.40.cloned.1.call-update) | async-done | bytes 1048592 | tf_op jit(solution)/shard_map/all_gather | solution.py:50
  684.8 1.5 reshape.148
  686.8 0.7 reshape.149
  687.5 74.7 %all-gather.42.cloned.1.call-done = bf16[64,2,4096]{2,1,0:T(2,128)(2,1)} async-done(((bf16[1,2,4096]{2,1,0:T(2,128)(2,1)}), bf16[64,2,4096]{2,1,0:T(2,128)(2,1)}) %all-gather.42.cloned.1.call-update) | async-done | bytes 1048592 | tf_op jit(solution)/shard_map/all_gather | solution.py:50
  762.2 1.5 reshape.150
  763.7 0.3 fusion.22
  764.2 0.7 reshape.151
  764.9 74.7 %all-gather.44.cloned.1.call-done = bf16[64,2,4096]{2,1,0:T(2,128)(2,1)} async-done(((bf16[1,2,4096]{2,1,0:T(2,128)(2,1)}), bf16[64,2,4096]{2,1,0:T(2,128)(2,1)}) %all-gather.44.cloned.1.call-update) | async-done | bytes 1048592 | tf_op jit(solution)/shard_map/all_gather | solution.py:50
  839.6 1.5 reshape.152
  841.0 0.3 fusion.23
  841.7 0.6 copy-done.6
  842.3 0.6 bitcast_dynamic-update-slice_fusion
  (69 shorter events, 6.1 us)
Async XLA Ops:
  6.5 52.2 %copy-start = (bf16[6,2,128,128]{3,2,1,0:T(8,128)(2,1)S(1)}, bf16[6,2,128,128]{3,2,1,0:T(8,128)(2,1)}, u32[]{:S(2)}) copy-start(bf16[6,2,128,128]{3,2,1,0:T(8,128)(2,1)} %param.10) | copy-start | bytes 1179652
  6.5 51.3 %all-reduce.8.cloned.1.call-start = ((), (), s32[]{:S(2)}) async-start(), calls=%async_computation | async-start | bytes 196608 | tf_op jit(solution)/shard_map/psum | solution.py:15
  7.3 133.8 %all-gather.26.cloned.1.call-start = ((), (), s32[]{:S(2)}) async-start(), calls=%async_computation.1 | async-start | bytes 1064960 | tf_op jit(solution)/shard_map/all_gather | solution.py:30
  61.2 157.9 %all-gather.28.cloned.1.call-start = ((), (), s32[]{:S(2)}) async-start(), calls=%async_computation.2 | async-start | bytes 1064960 | tf_op jit(solution)/shard_map/all_gather | solution.py:30
  61.2 0.7 copy-start.7
  62.5 0.7 copy-start.3
  142.5 0.9 copy-start.2
  142.6 1.0 copy-start.1
  144.4 152.1 %all-gather.30.cloned.1.call-start = ((), (), s32[]{:S(2)}) async-start(), calls=%async_computation.3 | async-start | bytes 1064960 | tf_op jit(solution)/shard_map/all_gather | solution.py:30
  221.8 152.1 %all-gather.32.cloned.1.call-start = ((), (), s32[]{:S(2)}) async-start(), calls=%async_computation.4 | async-start | bytes 1064960 | tf_op jit(solution)/shard_map/all_gather | solution.py:30
  299.2 152.1 %all-gather.34.cloned.1.call-start = ((), (), s32[]{:S(2)}) async-start(), calls=%async_computation.5 | async-start | bytes 1064960 | tf_op jit(solution)/shard_map/all_gather | solution.py:30
  376.6 152.8 %all-gather.36.cloned.1.call-start = ((), (), s32[]{:S(2)}) async-start(), calls=%async_computation.6 | async-start | bytes 1064960 | tf_op jit(solution)/shard_map/all_gather | solution.py:50
  452.8 1.0 copy-start.4
  454.7 152.8 %all-gather.38.cloned.1.call-start = ((), (), s32[]{:S(2)}) async-start(), calls=%async_computation.7 | async-start | bytes 1064960 | tf_op jit(solution)/shard_map/all_gather | solution.py:50
  530.8 1.0 copy-start.5
  532.7 152.1 %all-gather.40.cloned.1.call-start = ((), (), s32[]{:S(2)}) async-start(), calls=%async_computation.8 | async-start | bytes 1064960 | tf_op jit(solution)/shard_map/all_gather | solution.py:50
  610.1 152.1 %all-gather.42.cloned.1.call-start = ((), (), s32[]{:S(2)}) async-start(), calls=%async_computation.9 | async-start | bytes 1064960 | tf_op jit(solution)/shard_map/all_gather | solution.py:50
  687.5 152.1 %all-gather.44.cloned.1.call-start = ((), (), s32[]{:S(2)}) async-start(), calls=%async_computation.10 | async-start | bytes 1064960 | tf_op jit(solution)/shard_map/all_gather | solution.py:50
  841.7 0.6 copy-start.6
Sparse Core Ops, SparseCore 0:
  9.6 48.1 all-reduce.7
  61.3 79.7 all-gather.25
  144.5 74.5 all-gather.27
  221.9 74.5 all-gather.29
  299.3 74.5 all-gather.31
  376.7 74.5 all-gather.33
  454.8 74.5 all-gather.35
  532.8 74.5 all-gather.37
  610.2 74.5 all-gather.39
  687.6 74.5 all-gather.41
  765.0 74.5 all-gather.43
where the time goes:
time: 850 us; the launch traced here: 849 us
  waiting for transfers between devices  780 us (92%)
  local copies, waits for them, and re-layouts  27 us (3%)
  blocking collectives  19.4 us (2%)
  between operations  14.1 us (2%)
    all_gather x5, waiting for transfers between devices, on_device(): lax.all_gather(upper_flat, 'grid', axis=0, tiled=True)  373 us
    all_gather x5, waiting for transfers between devices, on_device(): values = lax.all_gather(sent, 'grid', axis=0, tiled=True)  356 us
    psum x1, waiting for transfers between devices, on_device(): lax.psum(lower_updates[0].astype(f32).astype(jnp.bfloat16), 'gz')  49.8 us
    unnamed x51, local copies, waits for them, and re-layouts  26.1 us
    unnamed x1, blocking collectives  19.4 us
  transfers between devices with their start and end apart: 11, of which 11 were waited for; matrix products, arithmetic and copies ran while one was open for 0% of the time, Pallas kernels for 0%

commit v1 on v0

v1 whole, which is shorter than its diff:
```python
import functools

import jax
import jax.numpy as jnp
from jax import lax
from jax.experimental import pallas as pl
from jax.experimental.pallas import tpu as pltpu
from jax.sharding import PartitionSpec as P

MESH = pl.DeviceIdType.MESH
F32 = jnp.float32
BF16 = jnp.bfloat16


def kernel(
    nx,
    ng,
    parent,
    live_count,
    rhs,
    upd,
    diag_hbm,
    lower_hbm,
    vinv_hbm,
    upper_hbm,
    out,
    diag,
    lower,
    vinv,
    upper,
    ml,
    uv,
    rhs_own,
    upd_all,
    fv,
    sol,
    build,
    up_in,
    downs,
    load_sem,
    rs_send,
    rs_recv,
    up_send,
    up_recv,
    down_send,
    down_recv,
    ag_send,
    ag_recv,
    own_sem,
):
    levels = rhs.shape[0]
    x = lax.axis_index("gz")
    g = lax.axis_index("grid")
    sizes = [min(ng, 4 * 2**l) for l in range(levels - 1)]

    barrier = pltpu.get_barrier_semaphore()

    def greet(j, c):
        other = lax.rem(g + 1 + j, ng)
        pl.semaphore_signal(barrier, inc=1, device_id=(x, other), device_id_type=MESH)
        return c

    lax.fori_loop(0, ng - 1, greet, 0)
    for k in range(1, nx):
        pl.semaphore_signal(
            barrier, inc=1, device_id=(lax.rem(x + k, nx), g), device_id_type=MESH
        )

    loads = [
        pltpu.make_async_copy(rhs.at[:, :, x], rhs_own, load_sem.at[0]),
        pltpu.make_async_copy(upd.at[:, :, x], upd_all.at[0], load_sem.at[1]),
        pltpu.make_async_copy(diag_hbm, diag, load_sem.at[2]),
        pltpu.make_async_copy(lower_hbm, lower, load_sem.at[3]),
        pltpu.make_async_copy(vinv_hbm, vinv, load_sem.at[4]),
        pltpu.make_async_copy(upper_hbm, upper, load_sem.at[5]),
    ]
    for c in loads:
        c.start()

    pl.semaphore_wait(barrier, ng - 1 + nx - 1)

    def rs_copies(part):
        span = pl.ds(0, 1) if part == 0 else pl.ds(1, levels - 1)
        return [
            pltpu.make_async_remote_copy(
                src_ref=upd.at[span, :, lax.rem(x + k, nx)],
                dst_ref=upd_all.at[k, span],
                send_sem=rs_send.at[k - 1, part],
                recv_sem=rs_recv.at[k - 1, part],
                device_id=(lax.rem(x + k, nx), g),
                device_id_type=MESH,
            )
            for k in range(1, nx)
        ]

    rs = [rs_copies(0), rs_copies(1)]
    for part in rs:
        for c in part:
            c.start()

    loads[2].wait()
    loads[3].wait()

    def products(a, b, dst, l):
        for s in range(2):
            m = jnp.dot(a[l, s], b[l, s], preferred_element_type=F32)
            dst[l, pl.ds(128 * s, 128), :] = m.astype(BF16)

    products(diag, lower, ml, 0)
    loads[4].wait()
    loads[5].wait()
    loads[0].wait()
    loads[1].wait()

    row = lax.broadcasted_iota(jnp.int32, (16, 128), 0)
    second = row >= 8
    slotrow = row // 8

    def spread(v):
        zero = jnp.zeros_like(v)
        return jnp.concatenate(
            [jnp.where(second, zero, v), jnp.where(second, v, zero)], axis=1
        ).astype(BF16)

    def live_of(l):
        return (slotrow < live_count[l, 0]).astype(F32)

    def mats(ref, l):
        return ref[l].reshape(256, 128)

    for c in rs[0]:
        c.wait_recv()

    incoming = None
    for l in range(levels):
        if l == 1:
            for c in rs[1]:
                c.wait_recv()
        total = rhs_own[l].astype(F32).reshape(16, 128)
        for k in range(nx):
            total = total - upd_all[k, l].astype(F32).reshape(16, 128)
        if incoming is not None:
            total = total - incoming
        live = live_of(l)
        res = spread(total)
        if l == levels - 1:
            fwd = jnp.dot(res, mats(diag, l), preferred_element_type=F32) * live
            top = jnp.dot(spread(fwd), mats(vinv, l), preferred_element_type=F32)
            sol[l] = (top * live).astype(BF16)
            break
        n = sizes[l]
        rel = lax.rem(g, n)
        base = g - rel
        sent = jnp.dot(res, ml[l], preferred_element_type=F32) * live
        a = jnp.concatenate([sent[:8], sent[:8]], axis=0)
        b = jnp.concatenate([sent[8:], sent[8:]], axis=0)
        pa = parent[l, 0] - 2 * base - slotrow
        pb = parent[l, 1] - 2 * base - slotrow
        zero = jnp.zeros_like(a)

        def tile(d):
            return (
                jnp.where(pa == 2 * d, a, zero) + jnp.where(pb == 2 * d, b, zero)
            ).astype(BF16)

        offset = sum(sizes[:l])
        for d in range(n):
            build[offset + d] = tile(d)
        own = tile(rel)

        def start(j, c, l=l, n=n, rel=rel, base=base, offset=offset):
            k = n // 2 + (1 - 2 * lax.rem(j, 2)) * ((j + 1) // 2)
            dest = lax.rem(rel + k, n)
            pltpu.make_async_remote_copy(
                src_ref=build.at[offset + dest],
                dst_ref=up_in.at[offset + k],
                send_sem=up_send.at[l],
                recv_sem=up_recv.at[l],
                device_id=(x, base + dest),
                device_id_type=MESH,
            ).start()
            return c

        lax.fori_loop(0, n - 1, start, 0)

        fwd = jnp.dot(res, mats(diag, l), preferred_element_type=F32) * live
        fv[l] = jnp.dot(spread(fwd), mats(vinv, l), preferred_element_type=F32)
        if l + 1 < levels - 1:
            products(diag, lower, ml, l + 1)
        products(upper, vinv, uv, l)

        whole = up_in.at[pl.ds(offset + 1, n - 1)]
        pltpu.make_async_copy(whole, whole, up_recv.at[l]).wait()
        incoming = own.astype(F32)
        for k in range(1, n):
            incoming = incoming + up_in[offset + k].astype(F32)

    def share(l):
        for k in range(1, nx):
            pltpu.make_async_remote_copy(
                src_ref=sol.at[l],
                dst_ref=out.at[l, x],
                send_sem=ag_send.at[0],
                recv_sem=ag_recv.at[0],
                device_id=(lax.rem(x + k, nx), g),
                device_id_type=MESH,
            ).start()
        pltpu.make_async_copy(sol.at[l], out.at[l, x], own_sem.at[l]).start()

    for l in range(levels - 2, -1, -1):
        n = sizes[l]
        rel = lax.rem(g, n)
        base = g - rel

        def start(j, c, l=l, n=n, rel=rel, base=base):
            k = n // 2 + (1 - 2 * lax.rem(j, 2)) * ((j + 1) // 2)
            dest = lax.rem(rel + k, n)
            pltpu.make_async_remote_copy(
                src_ref=sol.at[l + 1],
                dst_ref=downs[l].at[rel],
                send_sem=down_send.at[l],
                recv_sem=down_recv.at[l],
                device_id=(x, base + dest),
                device_id_type=MESH,
            ).start()
            return c

        lax.fori_loop(0, n - 1, start, 0)
        downs[l][rel] = sol[l + 1]
        share(l + 1)
        whole = downs[l].at[pl.ds(0, n - 1)]
        pltpu.make_async_copy(whole, whole, down_recv.at[l]).wait()
        picked = []
        for s in range(2):
            p = lax.rem(parent[l, s], 2 * n)
            t = downs[l][p // 2].astype(F32)
            picked.append(jnp.where(lax.rem(p, 2) == 0, t[:8], t[8:]))
        above = jnp.concatenate(picked, axis=0)
        low = jnp.dot(spread(above), uv[l], preferred_element_type=F32)
        sol[l] = ((fv[l] - low) * live_of(l)).astype(BF16)
    share(0)

    for part in rs:
        for c in part:
            c.wait_send()
    for l in range(levels - 1):
        n = sizes[l]
        offset = sum(sizes[:l])
        whole = up_in.at[pl.ds(offset, n - 1)]
        pltpu.make_async_copy(whole, whole, up_send.at[l]).wait()
        pltpu.make_async_copy(whole, whole, down_send.at[l]).wait()
    for l in range(levels):
        pltpu.make_async_copy(sol.at[l], out.at[l, x], own_sem.at[l]).wait()
    whole = out.at[:, pl.ds(0, nx - 1)]
    pltpu.make_async_copy(whole, whole, ag_send.at[0]).wait()
    pltpu.make_async_copy(whole, whole, ag_recv.at[0]).wait()


def solution(mesh):
    nx, ng = mesh.shape["gz"], mesh.shape["grid"]

    def on_device(rhs, upd, diag, lower, vinv, upper, parent, live_count):
        levels, slots, rows, width = rhs.shape
        part = rows // nx
        hbm = pl.BlockSpec(memory_space=pl.ANY)
        smem = pl.BlockSpec(memory_space=pltpu.SMEM)
        total = sum(min(ng, 4 * 2**l) for l in range(levels - 1))
        dma = pltpu.SemaphoreType.DMA
        result = pl.pallas_call(
            functools.partial(kernel, nx, ng),
            out_shape=jax.ShapeDtypeStruct((levels, nx, slots * part, width), BF16),
            in_specs=[smem, smem] + [hbm] * 6,
            out_specs=hbm,
            scratch_shapes=[
                pltpu.VMEM(diag.shape, BF16),
                pltpu.VMEM(lower.shape, BF16),
                pltpu.VMEM(vinv.shape, BF16),
                pltpu.VMEM(upper.shape, BF16),
                pltpu.VMEM((levels - 1, slots * width, width), BF16),
                pltpu.VMEM((levels - 1, slots * width, width), BF16),
                pltpu.VMEM((levels, slots, part, width), BF16),
                pltpu.VMEM((nx, levels, slots, part, width), BF16),
                pltpu.VMEM((levels - 1, slots * part, width), F32),
                pltpu.VMEM((levels, slots * part, width), BF16),
                pltpu.VMEM((total, slots * part, width), BF16),
                pltpu.VMEM((total, slots * part, width), BF16),
                [
                    pltpu.VMEM((min(ng, 4 * 2**l), slots * part, width), BF16)
                    for l in range(levels - 1)
                ],
                dma((6,)),
                dma((nx - 1, 2)),
                dma((nx - 1, 2)),
                dma((levels - 1,)),
                dma((levels - 1,)),
                dma((levels - 1,)),
                dma((levels - 1,)),
                dma((1,)),
                dma((1,)),
                dma((levels,)),
            ],
            compiler_params=pltpu.CompilerParams(
                collective_id=0, has_side_effects=True
            ),
        )(
            parent,
            live_count,
            rhs.reshape(levels, slots, nx, part, width),
            upd.reshape(levels, slots, nx, part, width),
            diag,
            lower,
            vinv,
            upper,
        )
        result = result.reshape(levels, nx, slots, part, width)
        return result.transpose(0, 2, 1, 3, 4).reshape(rhs.shape)

    return jax.shard_map(
        on_device,
        mesh=mesh,
        in_specs=(
            P(None, "grid", None, None),
            P("gz", None, "grid", None, None),
            P(None, "grid", None, None),
            P(None, "grid", None, None),
            P(None, "grid", None, None),
            P(None, "grid", None, None),
            P(None, "grid"),
            P(None, "grid"),
        ),
        out_specs=P(None, "grid", None, None),
        check_vma=False,
    )
```

time: 850 us -> 77.5 us (0.09)
  waiting for transfers between devices: 780 us -> 0 us
  Pallas kernels: 0 us -> 73.7 us
  local copies, waits for them, and re-layouts: 27 us -> 3.58 us
  blocking collectives: 19.4 us -> 0 us
  between operations: 14.1 us -> 0.01 us
    all_gather x10 -> x0, waiting for transfers between devices: 729 us -> none  [the longest x5 373 us: on_device(): lax.all_gather(upper_flat, 'grid', axis=0, tiled=True)]
    pallas_call x0 -> x1, Pallas kernels: none -> 73.7 us  [on_device(): pl.pallas_call(functools.partial(kernel, nx, ng), out_shape=jax.ShapeDtyp...]
    psum x1 -> x0, waiting for transfers between devices: 49.8 us -> none  [on_device(): lax.psum(lower_updates[0].astype(f32).astype(jnp.bfloat16), 'gz')]
    unnamed x51 -> x6, local copies, waits for them, and re-layouts: 26.1 us -> 2.03 us
    unnamed x1 -> x0, blocking collectives: 19.4 us -> none
  transfers between devices with their start and end apart: 11 -> 0, of which waited for: 11 -> 0; matrix products, arithmetic and copies ran while one was open for 0% -> 0% of each run, Pallas kernels for 0% -> 0%
where the time goes in v1:
time: 77.5 us; the launch traced here: 77.3 us
  Pallas kernels  73.7 us (95%)
  local copies, waits for them, and re-layouts  3.58 us (5%)
    pallas_call x1, Pallas kernels, on_device(): pl.pallas_call(functools.partial(kernel, nx, ng), out_shape=jax.ShapeDtyp...  73.7 us
    unnamed x6, local copies, waits for them, and re-layouts  2.03 us

profile of v1, /device:TPU:1, one launch (start us, length us, event | category | flops | bytes accessed | tf_op | source)
XLA Modules:
  0.0 77.3 jit_solution(494568196882459241)
XLA Ops:
  0.0 0.0 copy-start
  0.0 0.7 copy-done
  0.7 0.0 copy-start.1
  0.7 0.7 copy.9.parent
  1.4 0.0 copy-done.1
  1.4 0.7 copy.10.live_count
  2.0 73.7 %shard_map.82 = bf16[6,4,16,128]{3,2,1,0:T(8,128)(2,1)} custom-call(s32[5,2]{1,0:T(8,128)} %copy.9.parent, s32[6,1]{1,0:T(8,128)} %copy.10.live_count, bf16[6,2,4,8,128]{4,3,2,1,0:T(8,128)(2,1)} %bitcast.9, bf16[6,2,4,8,128]{4,3,2,1,0:T(8,128)(2,1)} %bitcast.10, bf16[6,2,128,128]{3,2,1,0:T(8,128)(2,1)} %diag_hbm.1, bf16[5,2,128,128]{3,2,1,0:T(8,128)(2,1)} %lower_hbm.1, ...), custom_call_target="tpu_custom_call" | custom-call | tf_op jit(solution)/shard_map/pallas_call | solution.py:269
  75.7 1.5 %copy_bitcast_fusion = bf16[6,2,32,128]{3,2,1,0:T(8,128)(2,1)} fusion(bf16[6,4,16,128]{3,2,1,0:T(8,128)(2,1)} %shard_map.82), kind=kLoop, calls=%fused_computation | loop fusion | bytes 196608 | tf_op jit(solution)/shard_map/reshape | solution.py:316
Async XLA Ops:
  0.0 0.7 copy-start
  0.7 0.7 copy-start.1

commit v2 on v0

v2 whole, which is shorter than its diff:
```python
import functools

import jax
import jax.numpy as jnp
from jax import lax
from jax.experimental import pallas as pl
from jax.experimental.pallas import tpu as pltpu
from jax.sharding import PartitionSpec as P

MESH = pl.DeviceIdType.MESH
F32 = jnp.float32
BF16 = jnp.bfloat16
NX, NY, NZ, NC = 4, 4, 8, 2
LEVELS = 6
CHIPS_Z = (2, 4, 8, 8, 8)
CHIPS_Y = (1, 1, 1, 2, 4)
SIZES = tuple(NC * a * b for a, b in zip(CHIPS_Z, CHIPS_Y))


def ring(k, n):
    return min(k, n - k)


def offsets(mz, my, cores):
    every = [
        (dy, dz, dc) for dy in range(my) for dz in range(mz) for dc in range(cores)
    ]
    every.sort(key=lambda o: -(ring(o[0], NY) + ring(o[1], NZ)))
    return [o for o in every if o != (0, 0, 0)]


def kernel(
    parent,
    live_count,
    rhs,
    upd,
    diag_hbm,
    lower_hbm,
    vinv_hbm,
    upper_hbm,
    out,
    diag,
    lower,
    vinv,
    upper,
    ml,
    uv_own,
    uv_part,
    tabs,
    ftabs,
    ids_own,
    ids,
    rhs_own,
    rhs_first,
    upd_first,
    upd_all,
    fv,
    sol,
    chain,
    build,
    build0,
    in0,
    ins,
    mate,
    top_tab,
    mid_tab,
    load_sem,
    send,
    recv,
    rs_send,
    rs_recv,
    tab_send,
    tab_recv,
    f_send,
    f_recv,
    own_sem,
):
    x = lax.axis_index("gz")
    g = lax.axis_index("grid")
    y, z, c = g // (NZ * NC), lax.rem(g // NC, NZ), lax.rem(g, NC)

    zs = {m: [z // m * m + lax.rem(z + k, m) for k in range(m)] for m in (2, 4, 8)}
    ys = {m: [y // m * m + lax.rem(y + k, m) for k in range(m)] for m in (1, 2, 4)}
    cs = [c, 1 - c]
    xs = [lax.rem(x + k, NX) for k in range(NX)]

    def at(off, mz, my):
        dy, dz, dc = off
        return (ys[my][dy] * NZ + zs[mz][dz]) * NC + cs[dc]

    def remote(src, dst, s, r, gx, gg):
        return pltpu.make_async_remote_copy(
            src_ref=src,
            dst_ref=dst,
            send_sem=s,
            recv_sem=r,
            device_id=(gx, gg),
            device_id_type=MESH,
        )

    def wait(view, sem):
        pltpu.make_async_copy(view, view, sem).wait()

    barrier = pltpu.get_barrier_semaphore()
    near = [(k, g) for k in xs[1:]]
    near += [(k, at(o, 2, 1)) for k in xs for o in offsets(2, 1, 2)]
    near += [(x, at((dy, 0, 0), 8, 4)) for dy in (1, 3)]
    far = [(0, dz, dc) for dz in (1, 2, 6, 7) for dc in (0, 1)]
    for gx, gg in near:
        pl.semaphore_signal(barrier, inc=1, device_id=(gx, gg), device_id_type=MESH)
    for o in far:
        pl.semaphore_signal(
            barrier, inc=1, device_id=(x, at(o, 8, 4)), device_id_type=MESH
        )

    loads = [
        pltpu.make_async_copy(upd.at[0], upd_first, load_sem.at[0]),
        pltpu.make_async_copy(rhs.at[0], rhs_first, load_sem.at[1]),
        pltpu.make_async_copy(diag_hbm, diag, load_sem.at[2]),
        pltpu.make_async_copy(lower_hbm, lower, load_sem.at[3]),
        pltpu.make_async_copy(vinv_hbm, vinv, load_sem.at[4]),
        pltpu.make_async_copy(upper_hbm, upper, load_sem.at[5]),
        pltpu.make_async_copy(rhs.at[:, :, x], rhs_own, load_sem.at[6]),
        pltpu.make_async_copy(upd.at[:, :, x], upd_all.at[0], load_sem.at[7]),
    ]
    for copy in loads:
        copy.start()
    for l in range(LEVELS - 1):
        for s in range(2):
            ids_own[0, 2 * l + s] = parent[s, l]

    row = lax.broadcasted_iota(jnp.int32, (16, 128), 0)
    slotrow = row // 8

    def spread(v, half):
        rows = lax.broadcasted_iota(jnp.int32, v.shape, 0)
        zero = jnp.zeros_like(v)
        return jnp.concatenate(
            [jnp.where(rows < half, v, zero), jnp.where(rows < half, zero, v)], axis=1
        ).astype(BF16)

    def live_of(l, rows=16):
        slot = lax.broadcasted_iota(jnp.int32, (rows, 128), 0) // (rows // 2)
        return (slot < live_count[0, l]).astype(F32)

    def dot(a, b):
        return jnp.dot(a, b, preferred_element_type=F32)

    def mats(ref, l):
        return ref[l].reshape(256, 128)

    def twice(v):
        return jnp.concatenate([v, v], axis=0)

    def target(p, n):
        return lax.rem(p, 2 * n) - slotrow

    def product(a, b, dst, l, place=None):
        for s in range(2):
            dst[l if place is None else place, pl.ds(128 * s, 128), :] = dot(
                a[l, s], b[l, s]
            ).astype(BF16)

    for k in range(4):
        loads[k].wait()
    first = rhs_first[...].astype(F32).reshape(64, 128) * (x == 0).astype(F32)
    first = first - upd_first[...].astype(F32).reshape(64, 128)
    f0 = dot(spread(first, 32), mats(diag, 0)) * live_of(0, 64)
    sent = dot(spread(f0, 32), mats(lower, 0))
    off0 = [(0, 0, 0)] + offsets(2, 1, 2)
    rels = [lax.rem(at(o, 2, 1), 4) for o in off0]
    pa, pb = target(parent[0, 0], 4), target(parent[1, 0], 4)
    for q in range(NX):
        a = twice(sent[8 * q : 8 * q + 8])
        b = twice(sent[32 + 8 * q : 40 + 8 * q])
        zero = jnp.zeros_like(a)
        for k, rel in enumerate(rels):
            build0[q, k] = (
                jnp.where(pa == 2 * rel, a, zero) + jnp.where(pb == 2 * rel, b, zero)
            ).astype(BF16)

    pl.semaphore_wait(barrier, len(near) + len(far))

    for dx in (2, 1, 3, 0):
        for k, o in enumerate(off0):
            if dx or k:
                remote(
                    build0.at[xs[dx], k],
                    in0.at[4 * dx + k],
                    send.at[0],
                    recv.at[0],
                    xs[dx],
                    at(o, 2, 1),
                ).start()
    rs = [
        remote(
            upd.at[:, :, xs[k]],
            upd_all.at[k],
            rs_send.at[k - 1],
            rs_recv.at[k - 1],
            xs[k],
            g,
        )
        for k in range(1, NX)
    ]
    for copy in rs:
        copy.start()

    for k in range(4, 8):
        loads[k].wait()
    part = pl.ds(32 * x, 32)
    for l in (1, 2, 3):
        for s in range(2):
            live = (s < live_count[0, l]).astype(F32)
            uv_part[l - 1, s] = (dot(upper[l, s, part, :], vinv[l, s]) * live).astype(
                BF16
            )

    def tab_first(l):
        nz = CHIPS_Z[l - 1]
        mine = lax.rem(z, nz)
        tab = tabs[l - 1]
        for o in offsets(nz, 1, 1):
            remote(
                uv_part.at[l - 1],
                tab.at[mine, c, :, x],
                tab_send.at[0, l - 1],
                tab_recv.at[0, l - 1],
                x,
                at(o, nz, 1),
            ).start()
        tab[mine, c, :, x] = uv_part[l - 1]

    def tab_first_wait(l):
        nz = CHIPS_Z[l - 1]
        wait(tabs[l - 1].at[pl.ds(0, nz - 1), 0, :, 0], tab_recv.at[0, l - 1])

    def tab_second(l):
        tab = tabs[l - 1]
        for k in (2, 1, 3):
            remote(
                tab.at[:, c, :, x],
                tab.at[:, c, :, x],
                tab_send.at[1, l - 1],
                tab_recv.at[1, l - 1],
                xs[k],
                g,
            ).start()

    def tab_second_wait(l):
        wait(tabs[l - 1].at[:, 0, :, pl.ds(0, NX - 1)], tab_recv.at[1, l - 1])

    def tab_third(l):
        tab = tabs[l - 1]
        remote(
            tab.at[:, c],
            tab.at[:, c],
            tab_send.at[2, l - 1],
            tab_recv.at[2, l - 1],
            x,
            at((0, 0, 1), 2, 1),
        ).start()

    def tab_third_wait(l):
        wait(tabs[l - 1].at[:, 0], tab_recv.at[2, l - 1])

    def f_share(l):
        n, nz = SIZES[l - 1], CHIPS_Z[l - 1]
        mine = lax.rem(g, n)
        tile = fv[l].astype(BF16)
        ftabs[l - 1][mine] = tile
        for o in offsets(nz, 1, 2):
            remote(
                ftabs[l - 1].at[mine],
                ftabs[l - 1].at[mine],
                f_send.at[l - 1],
                f_recv.at[l - 1],
                x,
                at(o, nz, 1),
            ).start()

    def forward(l, total):
        fwd = dot(spread(total, 8), mats(diag, l)) * live_of(l)
        fv[l] = dot(spread(fwd, 8), mats(vinv, l)) * live_of(l)

    def base(l):
        total = rhs_own[l].astype(F32).reshape(16, 128)
        for k in range(NX):
            total = total - upd_all[k, l].astype(F32).reshape(16, 128)
        return total

    product(diag, lower, ml, 1)
    tab_first(1)
    for copy in rs:
        copy.wait_recv()
    bases = base(1)
    wait(in0.at[pl.ds(1, 15)], recv.at[0])
    incoming = build0[x, 0].astype(F32)
    for k in range(1, 16):
        incoming = incoming + in0[k].astype(F32)

    for l in (1, 2, 3):
        n, mz, my = SIZES[l], CHIPS_Z[l], CHIPS_Y[l]
        total = bases - incoming
        sent = dot(spread(total, 8), ml[l]) * live_of(l)
        a, b = twice(sent[:8]), twice(sent[8:])
        zero = jnp.zeros_like(a)
        pa, pb = target(parent[0, l], n), target(parent[1, l], n)

        def tile(rel):
            return (
                jnp.where(pa == 2 * rel, a, zero) + jnp.where(pb == 2 * rel, b, zero)
            ).astype(BF16)

        offs = offsets(mz, my, 2)
        goals = [at(o, mz, my) for o in offs]
        start = sum(SIZES[1:l])
        for k, goal in enumerate(goals):
            build[start + k] = tile(lax.rem(goal, n))
        for k, goal in enumerate(goals):
            remote(
                build.at[start + k], ins[l - 1].at[k], send.at[l], recv.at[l], x, goal
            ).start()
        own = tile(lax.rem(g, n)).astype(F32)

        forward(l, total)
        f_share(l)
        product(diag, lower, ml, l + 1)
        if l == 1:
            tab_first(2)
            forward(0, base(0))
        if l == 2:
            tab_first(3)
            mine = lax.rem(g, 16)
            for s in range(10):
                ids[mine, s] = ids_own[0, s]
            for o in offsets(8, 1, 2):
                remote(
                    ids_own,
                    ids.at[pl.ds(mine, 1)],
                    send.at[8],
                    recv.at[8],
                    x,
                    at(o, 8, 1),
                ).start()
        if l == 3:
            for j in (1, 2, 3):
                tab_first_wait(j)
                tab_second(j)
            product(upper, vinv, uv_own, 0)
        bases = base(l + 1)
        wait(ins[l - 1].at[pl.ds(0, n - 1)], recv.at[l])
        incoming = own
        for k in range(n - 1):
            incoming = incoming + ins[l - 1][k].astype(F32)

    total = bases - incoming
    sent = dot(spread(total, 8), ml[4]) * live_of(4)
    partner = at((0, 0, 1), 2, 1)
    mate[0] = sent.astype(BF16)
    remote(mate.at[0], mate.at[1], send.at[5], recv.at[5], x, partner).start()
    wait(ids.at[pl.ds(0, 15)], recv.at[8])
    pa, pb = target(parent[0, 4], 64), target(parent[1, 4], 64)
    other = lax.rem(partner, 16)
    pc, pd = target(ids[other, 8], 64), target(ids[other, 9], 64)
    offs = offsets(8, 4, 1)
    goals = [at(o, 8, 4) for o in offs]
    a, b = twice(sent[:8]), twice(sent[8:])
    bases = base(5)
    wait(mate.at[1], recv.at[5])
    third = mate[1].astype(F32)
    d, e = twice(third[:8]), twice(third[8:])
    zero = jnp.zeros_like(a)

    def tile4(goal):
        return (
            jnp.where(pa == 2 * goal, a, zero)
            + jnp.where(pb == 2 * goal, b, zero)
            + jnp.where(pc == 2 * goal, d, zero)
            + jnp.where(pd == 2 * goal, e, zero)
        ).astype(BF16)

    start = sum(SIZES[1:4])
    for k, goal in enumerate(goals):
        build[start + k] = tile4(goal)
    for k, goal in enumerate(goals):
        remote(
            build.at[start + k], ins[3].at[k], send.at[4], recv.at[4], x, goal
        ).start()
    own = tile4(g).astype(F32)
    forward(4, total)
    product(upper, vinv, uv_own, 4, 1)
    for j in (1, 2, 3):
        tab_second_wait(j)
        tab_third(j)
    wait(ins[3].at[pl.ds(0, 31)], recv.at[4])
    incoming = own
    for k in range(31):
        incoming = incoming + ins[3][k].astype(F32)

    fwd = dot(spread(bases - incoming, 8), mats(diag, 5)) * live_of(5)
    sol[5] = (dot(spread(fwd, 8), mats(vinv, 5)) * live_of(5)).astype(BF16)

    def share(first, count):
        span = pl.ds(first, count)
        for k in (2, 1, 3):
            remote(
                sol.at[span], out.at[span, x], send.at[9], recv.at[9], xs[k], g
            ).start()
        pltpu.make_async_copy(
            sol.at[span], out.at[span, x], own_sem.at[first]
        ).start()

    def half(t, p):
        t = t.astype(F32)
        return jnp.where(lax.rem(p, 2) == 0, t[:8], t[8:])

    chip = y * NZ + z
    for o in offs:
        remote(
            sol.at[5], top_tab.at[chip, c], send.at[6], recv.at[6], x, at(o, 8, 4)
        ).start()
    top_tab[chip, c] = sol[5]
    share(5, 1)

    for j in (1, 2, 3):
        tab_third_wait(j)
        wait(ftabs[j - 1].at[pl.ds(0, SIZES[j - 1] - 1)], f_recv.at[j - 1])

    def tab_mat(l, p):
        return tabs[l - 1][p // 4, lax.rem(p // 2, 2), lax.rem(p, 2)].reshape(128, 128)

    ancestors = [[None, None] for _ in range(4)]
    for k in range(4):
        consts = []
        for s in range(2):
            own_p = [lax.rem(2 * g + s, 2 * SIZES[j - 1]) for j in range(1, 4)]
            path = {}
            p = parent[s, k]
            for j in range(k + 1, 4):
                n = SIZES[j - 1]
                q = lax.rem(p, 2 * n)
                path[j] = q
                p = ids[lax.rem(p // 2, 16), 2 * j + lax.rem(p, 2)]
            ancestors[k][s] = lax.rem(p, 64)
            if k > 0:
                path[k] = own_p[k - 1]
            m = const = None
            for j in range(3, k - 1, -1):
                if j == 0:
                    u = uv_own[0, pl.ds(128 * s, 128), :]
                else:
                    u = tab_mat(j, path[j])
                if j == k:
                    f = fv[k][8 * s : 8 * s + 8]
                else:
                    f = half(ftabs[j - 1][path[j] // 2], path[j])
                if m is None:
                    m, const = u, f
                else:
                    const = f - dot(const.astype(BF16), u)
                    m = dot(m, u).astype(BF16)
            chain[k, pl.ds(128 * s, 128), :] = m
            consts.append(const)
        fv[k] = jnp.concatenate(consts, axis=0)

    wait(top_tab.at[pl.ds(0, 31), 0], recv.at[6])
    remote(
        top_tab.at[:, c], top_tab.at[:, c], send.at[7], recv.at[7], x, partner
    ).start()
    wait(top_tab.at[:, 0], recv.at[7])
    above = jnp.concatenate(
        [
            half(top_tab[p // 4, lax.rem(p // 2, 2)], p)
            for p in (lax.rem(parent[0, 4], 128), lax.rem(parent[1, 4], 128))
        ],
        axis=0,
    )
    low = dot(spread(above, 8), uv_own[1])
    sol[4] = ((fv[4] - low) * live_of(4)).astype(BF16)

    mine = lax.rem(g, 32)
    offs = offsets(8, 2, 2)
    for o in offs:
        remote(
            sol.at[4], mid_tab.at[mine], send.at[10], recv.at[10], x, at(o, 8, 2)
        ).start()
    mid_tab[mine] = sol[4]
    share(4, 1)
    wait(mid_tab.at[pl.ds(0, 31)], recv.at[10])
    for k in range(4):
        above = jnp.concatenate(
            [half(mid_tab[p // 2], p) for p in ancestors[k]], axis=0
        )
        low = dot(spread(above, 8), chain[k])
        value = fv[k] - low if k % 2 == 1 else fv[k] + low
        sol[k] = (value * live_of(k)).astype(BF16)
    share(0, 4)

    wait(in0.at[pl.ds(1, 15)], send.at[0])
    for copy in rs:
        copy.wait_send()
    for l in (1, 2, 3):
        wait(ins[l - 1].at[pl.ds(0, SIZES[l] - 1)], send.at[l])
        nz = CHIPS_Z[l - 1]
        wait(tabs[l - 1].at[pl.ds(0, nz - 1), 0, :, 0], tab_send.at[0, l - 1])
        wait(tabs[l - 1].at[:, 0, :, pl.ds(0, NX - 1)], tab_send.at[1, l - 1])
        wait(tabs[l - 1].at[:, 0], tab_send.at[2, l - 1])
        wait(ftabs[l - 1].at[pl.ds(0, SIZES[l - 1] - 1)], f_send.at[l - 1])
    wait(ins[3].at[pl.ds(0, 31)], send.at[4])
    wait(mate.at[0], send.at[5])
    wait(top_tab.at[pl.ds(0, 31), 0], send.at[6])
    wait(top_tab.at[:, 0], send.at[7])
    wait(ids.at[pl.ds(0, 15)], send.at[8])
    wait(mid_tab.at[pl.ds(0, 31)], send.at[10])
    for first, count in ((5, 1), (4, 1), (0, 4)):
        span = pl.ds(first, count)
        pltpu.make_async_copy(
            sol.at[span], out.at[span, x], own_sem.at[first]
        ).wait()
    whole = out.at[:, pl.ds(0, NX - 1)]
    wait(whole, send.at[9])
    wait(whole, recv.at[9])


def solution(mesh):
    def on_device(rhs, upd, diag, lower, vinv, upper, parent, live_count):
        levels, slots, rows, width = rhs.shape
        part = rows // NX
        hbm = pl.BlockSpec(memory_space=pl.ANY)
        smem = pl.BlockSpec(memory_space=pltpu.SMEM)
        dma = pltpu.SemaphoreType.DMA
        pair = slots * width
        tile = (slots * part, width)
        split = (slots, NX, part, width)

        def vmem(*shape, dtype=BF16):
            return pltpu.VMEM(shape, dtype)

        result = pl.pallas_call(
            kernel,
            out_shape=jax.ShapeDtypeStruct((levels, NX) + tile, BF16),
            in_specs=[smem, smem] + [hbm] * 6,
            out_specs=hbm,
            scratch_shapes=[
                vmem(*diag.shape),
                vmem(*lower.shape),
                vmem(*vinv.shape),
                vmem(*upper.shape),
                vmem(levels - 1, pair, width),
                vmem(2, pair, width),
                vmem(3, slots, width // NX, width),
                [
                    vmem(CHIPS_Z[l], NC, slots, NX, width // NX, width)
                    for l in range(3)
                ],
                [vmem(SIZES[l], *tile) for l in range(3)],
                pltpu.SMEM((1, 128), jnp.int32),
                pltpu.SMEM((16, 128), jnp.int32),
                vmem(levels, slots, part, width),
                vmem(*split),
                vmem(*split),
                vmem(NX, levels, slots, part, width),
                vmem(levels - 1, *tile, dtype=F32),
                vmem(levels, *tile),
                vmem(4, pair, width),
                vmem(sum(SIZES[1:4]) + 32, *tile),
                vmem(NX, 4, *tile),
                vmem(16, *tile),
                [vmem(n, *tile) for n in (8, 16, 32, 32)],
                vmem(2, *tile),
                vmem(32, NC, *tile),
                vmem(32, *tile),
                dma((8,)),
                dma((11,)),
                dma((11,)),
                dma((NX - 1,)),
                dma((NX - 1,)),
                dma((3, 3)),
                dma((3, 3)),
                dma((3,)),
                dma((3,)),
                dma((levels,)),
            ],
            compiler_params=pltpu.CompilerParams(
                collective_id=0, has_side_effects=True
            ),
        )(
            parent.T,
            live_count.T,
            rhs.reshape(levels, slots, NX, part, width),
            upd.reshape(levels, slots, NX, part, width),
            diag,
            lower,
            vinv,
            upper,
        )
        result = result.reshape(levels, NX, slots, part, width)
        return result.transpose(0, 2, 1, 3, 4).reshape(rhs.shape)

    return jax.shard_map(
        on_device,
        mesh=mesh,
        in_specs=(
            P(None, "grid", None, None),
            P("gz", None, "grid", None, None),
            P(None, "grid", None, None),
            P(None, "grid", None, None),
            P(None, "grid", None, None),
            P(None, "grid", None, None),
            P(None, "grid"),
            P(None, "grid"),
        ),
        out_specs=P(None, "grid", None, None),
        check_vma=False,
    )
```

time: 850 us -> 56.1 us (0.07)
  waiting for transfers between devices: 780 us -> 0 us
  Pallas kernels: 0 us -> 54.4 us
  local copies, waits for them, and re-layouts: 27 us -> 1.55 us
  blocking collectives: 19.4 us -> 0 us
  between operations: 14.1 us -> 0.01 us
    all_gather x10 -> x0, waiting for transfers between devices: 729 us -> none  [the longest x5 373 us: on_device(): lax.all_gather(upper_flat, 'grid', axis=0, tiled=True)]
    pallas_call x0 -> x1, Pallas kernels: none -> 54.4 us  [on_device(): pl.pallas_call(kernel, out_shape=jax.ShapeDtypeStruct((levels, NX) + tile...]
    psum x1 -> x0, waiting for transfers between devices: 49.8 us -> none  [on_device(): lax.psum(lower_updates[0].astype(f32).astype(jnp.bfloat16), 'gz')]
    unnamed x51 -> x0, local copies, waits for them, and re-layouts: 26.1 us -> none
    unnamed x1 -> x0, blocking collectives: 19.4 us -> none
  transfers between devices with their start and end apart: 11 -> 0, of which waited for: 11 -> 0; matrix products, arithmetic and copies ran while one was open for 0% -> 0% of each run, Pallas kernels for 0% -> 0%
where the time goes in v2:
time: 56.1 us; the launch traced here: 56 us
  Pallas kernels  54.4 us (97%)
  local copies, waits for them, and re-layouts  1.55 us (3%)
    pallas_call x1, Pallas kernels, on_device(): pl.pallas_call(kernel, out_shape=jax.ShapeDtypeStruct((levels, NX) + tile...  54.4 us
    reshape x1, local copies, waits for them, and re-layouts, on_device(): return result.transpose(0, 2, 1, 3, 4).reshape(rhs.shape)  1.55 us

profile of v2, /device:TPU:1, one launch (start us, length us, event | category | flops | bytes accessed | tf_op | source)
XLA Modules:
  0.0 56.0 jit_solution(15084513569344825718)
XLA Ops:
  0.0 54.4 %shard_map.82 = bf16[6,4,16,128]{3,2,1,0:T(8,128)(2,1)} custom-call(s32[2,5]{1,0:T(2,128)} %bitcast.13, s32[1,6]{1,0:T(1,128)} %bitcast.14, bf16[6,2,4,8,128]{4,3,2,1,0:T(8,128)(2,1)} %bitcast.11, bf16[6,2,4,8,128]{4,3,2,1,0:T(8,128)(2,1)} %bitcast.12, bf16[6,2,128,128]{3,2,1,0:T(8,128)(2,1)} %diag_hbm.1, bf16[5,2,128,128]{3,2,1,0:T(8,128)(2,1)} %lower_hbm.1, ...), custom_call_target="tpu_custom_call" | custom-call | tf_op jit(solution)/shard_map/pallas_call | solution.py:540
  54.4 1.5 %copy_bitcast_fusion = bf16[6,2,32,128]{3,2,1,0:T(8,128)(2,1)} fusion(bf16[6,4,16,128]{3,2,1,0:T(8,128)(2,1)} %shard_map.82), kind=kLoop, calls=%fused_computation | loop fusion | bytes 196608 | tf_op jit(solution)/shard_map/reshape | solution.py:599

commit v3 on v2

--- a/solution.py
+++ b/solution.py
@@ -47,6 +47,7 @@
     uv_own,
     uv_part,
     tabs,
+    picks,
     ftabs,
     ids_own,
     ids,
@@ -63,7 +64,6 @@
     ins,
     mate,
     top_tab,
-    mid_tab,
     load_sem,
     send,
     recv,
@@ -71,6 +71,10 @@
     rs_recv,
     tab_send,
     tab_recv,
+    ring_send,
+    ring_recv,
+    pick_send,
+    pick_recv,
     f_send,
     f_recv,
     own_sem,
@@ -155,11 +159,9 @@
     def target(p, n):
         return lax.rem(p, 2 * n) - slotrow
 
-    def product(a, b, dst, l, place=None):
+    def product(a, b, dst, l):
         for s in range(2):
-            dst[l if place is None else place, pl.ds(128 * s, 128), :] = dot(
-                a[l, s], b[l, s]
-            ).astype(BF16)
+            dst[l, pl.ds(128 * s, 128), :] = dot(a[l, s], b[l, s]).astype(BF16)
 
     for k in range(4):
         loads[k].wait()
@@ -208,75 +210,113 @@
 
     for k in range(4, 8):
         loads[k].wait()
+    partner = at((0, 0, 1), 2, 1)
     part = pl.ds(32 * x, 32)
-    for l in (1, 2, 3):
+    up_row = lax.rem(y, 2)
+    homes = [lax.rem(z, 2), lax.rem(z, 4), z, up_row * NZ + z]
+
+    for l in (1, 2, 3, 4):
         for s in range(2):
             live = (s < live_count[0, l]).astype(F32)
-            uv_part[l - 1, s] = (dot(upper[l, s, part, :], vinv[l, s]) * live).astype(
-                BF16
-            )
-
-    def tab_first(l):
+            quarter = (dot(upper[l, s, part, :], vinv[l, s]) * live).astype(BF16)
+            uv_part[l - 1, s] = quarter
+            tabs[l - 1][homes[l - 1], c, s] = quarter
+
+    def table_direct(l):
         nz = CHIPS_Z[l - 1]
-        mine = lax.rem(z, nz)
-        tab = tabs[l - 1]
         for o in offsets(nz, 1, 1):
             remote(
                 uv_part.at[l - 1],
-                tab.at[mine, c, :, x],
+                tabs[l - 1].at[homes[l - 1], c],
                 tab_send.at[0, l - 1],
                 tab_recv.at[0, l - 1],
                 x,
                 at(o, nz, 1),
             ).start()
-        tab[mine, c, :, x] = uv_part[l - 1]
-
-    def tab_first_wait(l):
-        nz = CHIPS_Z[l - 1]
-        wait(tabs[l - 1].at[pl.ds(0, nz - 1), 0, :, 0], tab_recv.at[0, l - 1])
-
-    def tab_second(l):
-        tab = tabs[l - 1]
-        for k in (2, 1, 3):
-            remote(
-                tab.at[:, c, :, x],
-                tab.at[:, c, :, x],
-                tab_send.at[1, l - 1],
-                tab_recv.at[1, l - 1],
-                xs[k],
-                g,
-            ).start()
-
-    def tab_second_wait(l):
-        wait(tabs[l - 1].at[:, 0, :, pl.ds(0, NX - 1)], tab_recv.at[1, l - 1])
-
-    def tab_third(l):
+
+    def direct_view(l):
+        return tabs[l - 1].at[pl.ds(0, CHIPS_Z[l - 1] - 1), 0]
+
+    def table_ring(step):
+        for i, first in ((0, 0), (1, up_row * NZ)):
+            tab = tabs[2 + i]
+            if step == 3:
+                moves = [(z, (0, 4, 0))]
+            else:
+                moves = [
+                    (lax.rem(z + NZ - step, NZ), (0, 1, 0)),
+                    (lax.rem(z + step, NZ), (0, 7, 0)),
+                ]
+            for block, o in moves:
+                remote(
+                    tab.at[first + block, c] if step else uv_part.at[2 + i],
+                    tab.at[first + block, c],
+                    ring_send.at[i, step],
+                    ring_recv.at[i, step],
+                    x,
+                    at(o, 8, 1),
+                ).start()
+
+    def ring_view(i, step):
+        return tabs[2 + i].at[pl.ds(0, 1 if step == 3 else 2), 0]
+
+    def ring_wait(step):
+        for i in range(2):
+            wait(ring_view(i, step), ring_recv.at[i, step])
+
+    rows_view = tabs[3].at[pl.ds(up_row * NZ, NZ), c]
+
+    def rows_swap():
+        remote(
+            rows_view,
+            rows_view,
+            tab_send.at[0, 3],
+            tab_recv.at[0, 3],
+            x,
+            at((1, 0, 0), 8, 2),
+        ).start()
+
+    def core_swap(l):
         tab = tabs[l - 1]
         remote(
             tab.at[:, c],
             tab.at[:, c],
-            tab_send.at[2, l - 1],
-            tab_recv.at[2, l - 1],
+            tab_send.at[1, l - 1],
+            tab_recv.at[1, l - 1],
             x,
-            at((0, 0, 1), 2, 1),
+            partner,
         ).start()
 
-    def tab_third_wait(l):
-        wait(tabs[l - 1].at[:, 0], tab_recv.at[2, l - 1])
+    def core_view(l):
+        return tabs[l - 1].at[:, 0]
+
+    def pick_share(i):
+        for k in (2, 1, 3):
+            remote(
+                picks[i].at[:, x],
+                picks[i].at[:, x],
+                pick_send.at[i],
+                pick_recv.at[i],
+                xs[k],
+                g,
+            ).start()
+
+    def pick_view(i):
+        return picks[i].at[:, pl.ds(0, NX - 1)]
 
     def f_share(l):
-        n, nz = SIZES[l - 1], CHIPS_Z[l - 1]
+        n, nz, ny = SIZES[l - 1], CHIPS_Z[l - 1], CHIPS_Y[l - 1]
         mine = lax.rem(g, n)
         tile = fv[l].astype(BF16)
         ftabs[l - 1][mine] = tile
-        for o in offsets(nz, 1, 2):
+        for o in offsets(nz, ny, 2):
             remote(
                 ftabs[l - 1].at[mine],
                 ftabs[l - 1].at[mine],
                 f_send.at[l - 1],
                 f_recv.at[l - 1],
                 x,
-                at(o, nz, 1),
+                at(o, nz, ny),
             ).start()
 
     def forward(l, total):
@@ -289,8 +329,9 @@
             total = total - upd_all[k, l].astype(F32).reshape(16, 128)
         return total
 
+    table_direct(1)
+    table_ring(0)
     product(diag, lower, ml, 1)
-    tab_first(1)
     for copy in rs:
         copy.wait_recv()
     bases = base(1)
@@ -325,13 +366,13 @@
 
         forward(l, total)
         f_share(l)
-        product(diag, lower, ml, l + 1)
         if l == 1:
-            tab_first(2)
+            table_direct(2)
+            ring_wait(0)
+            table_ring(1)
             forward(0, base(0))
         if l == 2:
-            tab_first(3)
-            mine = lax.rem(g, 16)
+            mine = lax.rem(g, 32)
             for s in range(10):
                 ids[mine, s] = ids_own[0, s]
             for o in offsets(8, 1, 2):
@@ -343,11 +384,54 @@
                     x,
                     at(o, 8, 1),
                 ).start()
+            ring_wait(1)
+            table_ring(2)
+            table_ring(3)
+            for j in (1, 2):
+                wait(direct_view(j), tab_recv.at[0, j - 1])
+                core_swap(j)
+        if l == 3:
+            ring_wait(2)
+            ring_wait(3)
+            rows_swap()
+            core_swap(3)
+            wait(ids.at[pl.ds(0, 15)], recv.at[8])
+            half_ids = ids.at[pl.ds(16 * up_row, 16)]
+            remote(
+                half_ids, half_ids, send.at[7], recv.at[7], x, at((1, 0, 0), 8, 2)
+            ).start()
+        product(diag, lower, ml, l + 1)
+        product(upper, vinv, uv_own, l)
         if l == 3:
             for j in (1, 2, 3):
-                tab_first_wait(j)
-                tab_second(j)
-            product(upper, vinv, uv_own, 0)
+                wait(core_view(j), tab_recv.at[1, j - 1])
+            wait(half_ids, recv.at[7])
+            chains = []
+            for k in range(4):
+                for s in range(2):
+                    path = {}
+                    p = parent[s, k]
+                    for j in range(k + 1, 5):
+                        n = SIZES[j - 1]
+                        path[j] = lax.rem(p, 2 * n)
+                        p = ids[
+                            lax.rem(path[j] // 2, n) + (g // n * n - g // 32 * 32),
+                            2 * j + lax.rem(path[j], 2),
+                        ]
+                    path[5] = lax.rem(p, 128)
+                    chains.append(path)
+            places = {}
+            for k in range(3):
+                for s in range(2):
+                    for j in range(k + 1, 4):
+                        p = chains[2 * k + s][j]
+                        places[k, s, j] = len(places)
+                        picks[0][places[k, s, j], x] = tabs[j - 1][
+                            p // 4, lax.rem(p // 2, 2), lax.rem(p, 2)
+                        ]
+            pick_share(0)
+            wait(rows_view, tab_recv.at[0, 3])
+            core_swap(4)
         bases = base(l + 1)
         wait(ins[l - 1].at[pl.ds(0, n - 1)], recv.at[l])
         incoming = own
@@ -356,12 +440,10 @@
 
     total = bases - incoming
     sent = dot(spread(total, 8), ml[4]) * live_of(4)
-    partner = at((0, 0, 1), 2, 1)
     mate[0] = sent.astype(BF16)
     remote(mate.at[0], mate.at[1], send.at[5], recv.at[5], x, partner).start()
-    wait(ids.at[pl.ds(0, 15)], recv.at[8])
     pa, pb = target(parent[0, 4], 64), target(parent[1, 4], 64)
-    other = lax.rem(partner, 16)
+    other = lax.rem(partner, 32)
     pc, pd = target(ids[other, 8], 64), target(ids[other, 9], 64)
     offs = offsets(8, 4, 1)
     goals = [at(o, 8, 4) for o in offs]
@@ -388,11 +470,45 @@
             build.at[start + k], ins[3].at[k], send.at[4], recv.at[4], x, goal
         ).start()
     own = tile4(g).astype(F32)
+    wait(core_view(4), tab_recv.at[1, 3])
+    for k in range(4):
+        for s in range(2):
+            p = chains[2 * k + s][4]
+            picks[1][2 * k + s, x] = tabs[3][p // 4, lax.rem(p // 2, 2), lax.rem(p, 2)]
+    pick_share(1)
     forward(4, total)
-    product(upper, vinv, uv_own, 4, 1)
+    f_share(4)
+    product(upper, vinv, uv_own, 4)
+    product(upper, vinv, uv_own, 0)
+
+    wait(pick_view(0), pick_recv.at[0])
     for j in (1, 2, 3):
-        tab_second_wait(j)
-        tab_third(j)
+        wait(ftabs[j - 1].at[pl.ds(0, SIZES[j - 1] - 1)], f_recv.at[j - 1])
+
+    def half(t, p):
+        t = t.astype(F32)
+        return jnp.where(lax.rem(p, 2) == 0, t[:8], t[8:])
+
+    for k in range(4):
+        consts = []
+        for s in range(2):
+            path = chains[2 * k + s]
+            m = const = None
+            for j in range(3, k - 1, -1):
+                if j == k:
+                    u = uv_own[k, pl.ds(128 * s, 128), :]
+                    f = fv[k, pl.ds(8 * s, 8), :]
+                else:
+                    u = picks[0][places[k, s, j]].reshape(128, 128)
+                    f = half(ftabs[j - 1][path[j] // 2], path[j])
+                if m is None:
+                    m, const = u, f
+                else:
+                    const = f - dot(const.astype(BF16), u)
+                    m = dot(m, u).astype(BF16)
+            chain[k, pl.ds(128 * s, 128), :] = m
+            consts.append(const)
+        fv[k] = jnp.concatenate(consts, axis=0)
     wait(ins[3].at[pl.ds(0, 31)], recv.at[4])
     incoming = own
     for k in range(31):
@@ -411,10 +527,6 @@
             sol.at[span], out.at[span, x], own_sem.at[first]
         ).start()
 
-    def half(t, p):
-        t = t.astype(F32)
-        return jnp.where(lax.rem(p, 2) == 0, t[:8], t[8:])
-
     chip = y * NZ + z
     for o in offs:
         remote(
@@ -423,97 +535,61 @@
     top_tab[chip, c] = sol[5]
     share(5, 1)
 
-    for j in (1, 2, 3):
-        tab_third_wait(j)
-        wait(ftabs[j - 1].at[pl.ds(0, SIZES[j - 1] - 1)], f_recv.at[j - 1])
-
-    def tab_mat(l, p):
-        return tabs[l - 1][p // 4, lax.rem(p // 2, 2), lax.rem(p, 2)].reshape(128, 128)
-
-    ancestors = [[None, None] for _ in range(4)]
+    wait(pick_view(1), pick_recv.at[1])
+    wait(ftabs[3].at[pl.ds(0, 31)], f_recv.at[3])
     for k in range(4):
-        consts = []
+        sign = 1 if k % 2 == 0 else -1
+        ends = [chains[2 * k + s][4] for s in range(2)]
+        f = jnp.concatenate([half(ftabs[3][p // 2], p) for p in ends], axis=0)
+        fv[k] = fv[k] + sign * dot(spread(f, 8), chain[k])
         for s in range(2):
-            own_p = [lax.rem(2 * g + s, 2 * SIZES[j - 1]) for j in range(1, 4)]
-            path = {}
-            p = parent[s, k]
-            for j in range(k + 1, 4):
-                n = SIZES[j - 1]
-                q = lax.rem(p, 2 * n)
-                path[j] = q
-                p = ids[lax.rem(p // 2, 16), 2 * j + lax.rem(p, 2)]
-            ancestors[k][s] = lax.rem(p, 64)
-            if k > 0:
-                path[k] = own_p[k - 1]
-            m = const = None
-            for j in range(3, k - 1, -1):
-                if j == 0:
-                    u = uv_own[0, pl.ds(128 * s, 128), :]
-                else:
-                    u = tab_mat(j, path[j])
-                if j == k:
-                    f = fv[k][8 * s : 8 * s + 8]
-                else:
-                    f = half(ftabs[j - 1][path[j] // 2], path[j])
-                if m is None:
-                    m, const = u, f
-                else:
-                    const = f - dot(const.astype(BF16), u)
-                    m = dot(m, u).astype(BF16)
-            chain[k, pl.ds(128 * s, 128), :] = m
-            consts.append(const)
-        fv[k] = jnp.concatenate(consts, axis=0)
+            span = pl.ds(128 * s, 128)
+            u = picks[1][2 * k + s].reshape(128, 128)
+            chain[k, span, :] = dot(u, chain[k, span, :]).astype(BF16)
+    for s in range(2):
+        chain[4, pl.ds(128 * s, 128), :] = uv_own[4, pl.ds(128 * s, 128), :]
 
     wait(top_tab.at[pl.ds(0, 31), 0], recv.at[6])
     remote(
-        top_tab.at[:, c], top_tab.at[:, c], send.at[7], recv.at[7], x, partner
+        top_tab.at[:, c], top_tab.at[:, c], send.at[10], recv.at[10], x, partner
     ).start()
-    wait(top_tab.at[:, 0], recv.at[7])
-    above = jnp.concatenate(
-        [
-            half(top_tab[p // 4, lax.rem(p // 2, 2)], p)
-            for p in (lax.rem(parent[0, 4], 128), lax.rem(parent[1, 4], 128))
-        ],
-        axis=0,
-    )
-    low = dot(spread(above, 8), uv_own[1])
-    sol[4] = ((fv[4] - low) * live_of(4)).astype(BF16)
-
-    mine = lax.rem(g, 32)
-    offs = offsets(8, 2, 2)
-    for o in offs:
-        remote(
-            sol.at[4], mid_tab.at[mine], send.at[10], recv.at[10], x, at(o, 8, 2)
-        ).start()
-    mid_tab[mine] = sol[4]
-    share(4, 1)
-    wait(mid_tab.at[pl.ds(0, 31)], recv.at[10])
-    for k in range(4):
+    wait(top_tab.at[:, 0], recv.at[10])
+    for k in range(5):
+        if k < 4:
+            ends = [chains[2 * k + s][5] for s in range(2)]
+        else:
+            ends = [lax.rem(parent[s, 4], 128) for s in range(2)]
         above = jnp.concatenate(
-            [half(mid_tab[p // 2], p) for p in ancestors[k]], axis=0
+            [half(top_tab[p // 4, lax.rem(p // 2, 2)], p) for p in ends], axis=0
         )
         low = dot(spread(above, 8), chain[k])
-        value = fv[k] - low if k % 2 == 1 else fv[k] + low
+        value = fv[k] + low if k % 2 == 1 else fv[k] - low
         sol[k] = (value * live_of(k)).astype(BF16)
-    share(0, 4)
+    share(0, 5)
 
     wait(in0.at[pl.ds(1, 15)], send.at[0])
     for copy in rs:
         copy.wait_send()
     for l in (1, 2, 3):
         wait(ins[l - 1].at[pl.ds(0, SIZES[l] - 1)], send.at[l])
-        nz = CHIPS_Z[l - 1]
-        wait(tabs[l - 1].at[pl.ds(0, nz - 1), 0, :, 0], tab_send.at[0, l - 1])
-        wait(tabs[l - 1].at[:, 0, :, pl.ds(0, NX - 1)], tab_send.at[1, l - 1])
-        wait(tabs[l - 1].at[:, 0], tab_send.at[2, l - 1])
+        if l < 3:
+            wait(direct_view(l), tab_send.at[0, l - 1])
+    for step in range(4):
+        for i in range(2):
+            wait(ring_view(i, step), ring_send.at[i, step])
+    wait(rows_view, tab_send.at[0, 3])
+    for l in (1, 2, 3, 4):
+        wait(core_view(l), tab_send.at[1, l - 1])
         wait(ftabs[l - 1].at[pl.ds(0, SIZES[l - 1] - 1)], f_send.at[l - 1])
+    for i in range(2):
+        wait(pick_view(i), pick_send.at[i])
     wait(ins[3].at[pl.ds(0, 31)], send.at[4])
     wait(mate.at[0], send.at[5])
     wait(top_tab.at[pl.ds(0, 31), 0], send.at[6])
-    wait(top_tab.at[:, 0], send.at[7])
+    wait(half_ids, send.at[7])
     wait(ids.at[pl.ds(0, 15)], send.at[8])
-    wait(mid_tab.at[pl.ds(0, 31)], send.at[10])
-    for first, count in ((5, 1), (4, 1), (0, 4)):
+    wait(top_tab.at[:, 0], send.at[10])
+    for first, count in ((5, 1), (0, 5)):
         span = pl.ds(first, count)
         pltpu.make_async_copy(
             sol.at[span], out.at[span, x], own_sem.at[first]
@@ -548,38 +624,39 @@
                 vmem(*vinv.shape),
                 vmem(*upper.shape),
                 vmem(levels - 1, pair, width),
-                vmem(2, pair, width),
-                vmem(3, slots, width // NX, width),
-                [
-                    vmem(CHIPS_Z[l], NC, slots, NX, width // NX, width)
-                    for l in range(3)
-                ],
-                [vmem(SIZES[l], *tile) for l in range(3)],
+                vmem(levels - 1, pair, width),
+                vmem(4, slots, width // NX, width),
+                [vmem(SIZES[l] // NC, NC, slots, width // NX, width) for l in range(4)],
+                [vmem(n, NX, width // NX, width) for n in (12, 8)],
+                [vmem(SIZES[l], *tile) for l in range(4)],
                 pltpu.SMEM((1, 128), jnp.int32),
-                pltpu.SMEM((16, 128), jnp.int32),
+                pltpu.SMEM((32, 128), jnp.int32),
                 vmem(levels, slots, part, width),
                 vmem(*split),
                 vmem(*split),
                 vmem(NX, levels, slots, part, width),
                 vmem(levels - 1, *tile, dtype=F32),
                 vmem(levels, *tile),
-                vmem(4, pair, width),
+                vmem(levels - 1, pair, width),
                 vmem(sum(SIZES[1:4]) + 32, *tile),
                 vmem(NX, 4, *tile),
                 vmem(16, *tile),
                 [vmem(n, *tile) for n in (8, 16, 32, 32)],
                 vmem(2, *tile),
                 vmem(32, NC, *tile),
-                vmem(32, *tile),
                 dma((8,)),
                 dma((11,)),
                 dma((11,)),
                 dma((NX - 1,)),
                 dma((NX - 1,)),
-                dma((3, 3)),
-                dma((3, 3)),
-                dma((3,)),
-                dma((3,)),
+                dma((2, 4)),
+                dma((2, 4)),
+                dma((2, 4)),
+                dma((2, 4)),
+                dma((2,)),
+                dma((2,)),
+                dma((4,)),
+                dma((4,)),
                 dma((levels,)),
             ],
             compiler_params=pltpu.CompilerParams(

time: 56.1 us -> 53.8 us (0.959)
  Pallas kernels: 54.4 us -> 52.1 us
    pallas_call x1, Pallas kernels: 54.4 us -> 52.1 us  [on_device(): pl.pallas_call(kernel, out_shape=jax.ShapeDtypeStruct((levels, NX) + tile...]
where the time goes in v3:
time: 53.8 us; the launch traced here: 53.7 us
  Pallas kernels  52.1 us (97%)
  local copies, waits for them, and re-layouts  1.55 us (3%)
    pallas_call x1, Pallas kernels, on_device(): pl.pallas_call(kernel, out_shape=jax.ShapeDtypeStruct((levels, NX) + tile...  52.1 us
    reshape x1, local copies, waits for them, and re-layouts, on_device(): return result.transpose(0, 2, 1, 3, 4).reshape(rhs.shape)  1.55 us

profile of v3, /device:TPU:1, one launch (start us, length us, event | category | flops | bytes accessed | tf_op | source)
XLA Modules:
  0.0 53.7 jit_solution(14310463512152237500)
XLA Ops:
  0.0 52.1 %shard_map.82 = bf16[6,4,16,128]{3,2,1,0:T(8,128)(2,1)} custom-call(s32[2,5]{1,0:T(2,128)} %bitcast.13, s32[1,6]{1,0:T(1,128)} %bitcast.14, bf16[6,2,4,8,128]{4,3,2,1,0:T(8,128)(2,1)} %bitcast.11, bf16[6,2,4,8,128]{4,3,2,1,0:T(8,128)(2,1)} %bitcast.12, bf16[6,2,128,128]{3,2,1,0:T(8,128)(2,1)} %diag_hbm.1, bf16[5,2,128,128]{3,2,1,0:T(8,128)(2,1)} %lower_hbm.1, ...), custom_call_target="tpu_custom_call" | custom-call | tf_op jit(solution)/shard_map/pallas_call | solution.py:616
  52.1 1.5 %copy_bitcast_fusion = bf16[6,2,32,128]{3,2,1,0:T(8,128)(2,1)} fusion(bf16[6,4,16,128]{3,2,1,0:T(8,128)(2,1)} %shard_map.82), kind=kLoop, calls=%fused_computation | loop fusion | bytes 196608 | tf_op jit(solution)/shard_map/reshape | solution.py:676

commit v4 on v3

--- a/solution.py
+++ b/solution.py
@@ -73,6 +73,8 @@
     tab_recv,
     ring_send,
     ring_recv,
+    swap_send,
+    swap_recv,
     pick_send,
     pick_recv,
     f_send,
@@ -264,17 +266,22 @@
         for i in range(2):
             wait(ring_view(i, step), ring_recv.at[i, step])
 
-    rows_view = tabs[3].at[pl.ds(up_row * NZ, NZ), c]
-
-    def rows_swap():
-        remote(
-            rows_view,
-            rows_view,
-            tab_send.at[0, 3],
-            tab_recv.at[0, 3],
-            x,
-            at((1, 0, 0), 8, 2),
-        ).start()
+    swaps = ((0, 1, 7), (2, 6), (3, 5, 4))
+
+    def rows_swap(step):
+        for k in swaps[step]:
+            block = tabs[3].at[up_row * NZ + zs[8][k], c]
+            remote(
+                block,
+                block,
+                swap_send.at[step],
+                swap_recv.at[step],
+                x,
+                at((1, 0, 0), 8, 2),
+            ).start()
+
+    def rows_view(step):
+        return tabs[3].at[pl.ds(0, len(swaps[step])), 0]
 
     def core_swap(l):
         tab = tabs[l - 1]
@@ -305,19 +312,43 @@
         return picks[i].at[:, pl.ds(0, NX - 1)]
 
     def f_share(l):
-        n, nz, ny = SIZES[l - 1], CHIPS_Z[l - 1], CHIPS_Y[l - 1]
-        mine = lax.rem(g, n)
-        tile = fv[l].astype(BF16)
-        ftabs[l - 1][mine] = tile
-        for o in offsets(nz, ny, 2):
+        nz, ny = CHIPS_Z[l - 1], CHIPS_Y[l - 1]
+        tab = ftabs[l - 1]
+        tab[homes[l - 1], c] = fv[l].astype(BF16)
+        for o in offsets(nz, ny, 1):
             remote(
-                ftabs[l - 1].at[mine],
-                ftabs[l - 1].at[mine],
-                f_send.at[l - 1],
-                f_recv.at[l - 1],
+                tab.at[homes[l - 1], c],
+                tab.at[homes[l - 1], c],
+                f_send.at[0, l - 1],
+                f_recv.at[0, l - 1],
                 x,
                 at(o, nz, ny),
             ).start()
+
+    def f_view(l):
+        return ftabs[l - 1].at[pl.ds(0, SIZES[l - 1] // NC - 1), 0]
+
+    def f_swap(l):
+        wait(f_view(l), f_recv.at[0, l - 1])
+        tab = ftabs[l - 1]
+        remote(
+            tab.at[:, c],
+            tab.at[:, c],
+            f_send.at[1, l - 1],
+            f_recv.at[1, l - 1],
+            x,
+            partner,
+        ).start()
+
+    def f_wait(l):
+        wait(ftabs[l - 1].at[:, 0], f_recv.at[1, l - 1])
+
+    def f_tile(l, p):
+        return half(ftabs[l - 1][p // 4, lax.rem(p // 2, 2)], p)
+
+    def half(t, p):
+        t = t.astype(F32)
+        return jnp.where(lax.rem(p, 2) == 0, t[:8], t[8:])
 
     def forward(l, total):
         fwd = dot(spread(total, 8), mats(diag, l)) * live_of(l)
@@ -370,6 +401,7 @@
             table_direct(2)
             ring_wait(0)
             table_ring(1)
+            rows_swap(0)
             forward(0, base(0))
         if l == 2:
             mine = lax.rem(g, 32)
@@ -387,13 +419,14 @@
             ring_wait(1)
             table_ring(2)
             table_ring(3)
+            rows_swap(1)
             for j in (1, 2):
                 wait(direct_view(j), tab_recv.at[0, j - 1])
                 core_swap(j)
         if l == 3:
             ring_wait(2)
             ring_wait(3)
-            rows_swap()
+            rows_swap(2)
             core_swap(3)
             wait(ids.at[pl.ds(0, 15)], recv.at[8])
             half_ids = ids.at[pl.ds(16 * up_row, 16)]
@@ -430,8 +463,6 @@
                             p // 4, lax.rem(p // 2, 2), lax.rem(p, 2)
                         ]
             pick_share(0)
-            wait(rows_view, tab_recv.at[0, 3])
-            core_swap(4)
         bases = base(l + 1)
         wait(ins[l - 1].at[pl.ds(0, n - 1)], recv.at[l])
         incoming = own
@@ -470,25 +501,25 @@
             build.at[start + k], ins[3].at[k], send.at[4], recv.at[4], x, goal
         ).start()
     own = tile4(g).astype(F32)
+    for j in (1, 2, 3):
+        f_swap(j)
+    for step in range(3):
+        wait(rows_view(step), swap_recv.at[step])
+    core_swap(4)
+    forward(4, total)
+    f_share(4)
+    product(upper, vinv, uv_own, 4)
+    product(upper, vinv, uv_own, 0)
     wait(core_view(4), tab_recv.at[1, 3])
     for k in range(4):
         for s in range(2):
             p = chains[2 * k + s][4]
             picks[1][2 * k + s, x] = tabs[3][p // 4, lax.rem(p // 2, 2), lax.rem(p, 2)]
     pick_share(1)
-    forward(4, total)
-    f_share(4)
-    product(upper, vinv, uv_own, 4)
-    product(upper, vinv, uv_own, 0)
 
     wait(pick_view(0), pick_recv.at[0])
     for j in (1, 2, 3):
-        wait(ftabs[j - 1].at[pl.ds(0, SIZES[j - 1] - 1)], f_recv.at[j - 1])
-
-    def half(t, p):
-        t = t.astype(F32)
-        return jnp.where(lax.rem(p, 2) == 0, t[:8], t[8:])
-
+        f_wait(j)
     for k in range(4):
         consts = []
         for s in range(2):
@@ -500,7 +531,7 @@
                     f = fv[k, pl.ds(8 * s, 8), :]
                 else:
                     u = picks[0][places[k, s, j]].reshape(128, 128)
-                    f = half(ftabs[j - 1][path[j] // 2], path[j])
+                    f = f_tile(j, path[j])
                 if m is None:
                     m, const = u, f
                 else:
@@ -535,12 +566,13 @@
     top_tab[chip, c] = sol[5]
     share(5, 1)
 
+    f_swap(4)
     wait(pick_view(1), pick_recv.at[1])
-    wait(ftabs[3].at[pl.ds(0, 31)], f_recv.at[3])
+    f_wait(4)
     for k in range(4):
         sign = 1 if k % 2 == 0 else -1
         ends = [chains[2 * k + s][4] for s in range(2)]
-        f = jnp.concatenate([half(ftabs[3][p // 2], p) for p in ends], axis=0)
+        f = jnp.concatenate([f_tile(4, p) for p in ends], axis=0)
         fv[k] = fv[k] + sign * dot(spread(f, 8), chain[k])
         for s in range(2):
             span = pl.ds(128 * s, 128)
@@ -577,10 +609,12 @@
     for step in range(4):
         for i in range(2):
             wait(ring_view(i, step), ring_send.at[i, step])
-    wait(rows_view, tab_send.at[0, 3])
+    for step in range(3):
+        wait(rows_view(step), swap_send.at[step])
     for l in (1, 2, 3, 4):
         wait(core_view(l), tab_send.at[1, l - 1])
-        wait(ftabs[l - 1].at[pl.ds(0, SIZES[l - 1] - 1)], f_send.at[l - 1])
+        wait(f_view(l), f_send.at[0, l - 1])
+        wait(ftabs[l - 1].at[:, 0], f_send.at[1, l - 1])
     for i in range(2):
         wait(pick_view(i), pick_send.at[i])
     wait(ins[3].at[pl.ds(0, 31)], send.at[4])
@@ -628,7 +662,7 @@
                 vmem(4, slots, width // NX, width),
                 [vmem(SIZES[l] // NC, NC, slots, width // NX, width) for l in range(4)],
                 [vmem(n, NX, width // NX, width) for n in (12, 8)],
-                [vmem(SIZES[l], *tile) for l in range(4)],
+                [vmem(SIZES[l] // NC, NC, *tile) for l in range(4)],
                 pltpu.SMEM((1, 128), jnp.int32),
                 pltpu.SMEM((32, 128), jnp.int32),
                 vmem(levels, slots, part, width),
@@ -653,10 +687,12 @@
                 dma((2, 4)),
                 dma((2, 4)),
                 dma((2, 4)),
+                dma((3,)),
+                dma((3,)),
                 dma((2,)),
                 dma((2,)),
-                dma((4,)),
-                dma((4,)),
+                dma((2, 4)),
+                dma((2, 4)),
                 dma((levels,)),
             ],
             compiler_params=pltpu.CompilerParams(

time: 53.8 us -> 52.3 us (0.972)
  Pallas kernels: 52.1 us -> 50.5 us
    pallas_call x1, Pallas kernels: 52.1 us -> 50.5 us  [on_device(): pl.pallas_call(kernel, out_shape=jax.ShapeDtypeStruct((levels, NX) + tile...]
where the time goes in v4:
time: 52.3 us; the launch traced here: 52.1 us
  Pallas kernels  50.5 us (97%)
  local copies, waits for them, and re-layouts  1.55 us (3%)
    pallas_call x1, Pallas kernels, on_device(): pl.pallas_call(kernel, out_shape=jax.ShapeDtypeStruct((levels, NX) + tile...  50.5 us
    reshape x1, local copies, waits for them, and re-layouts, on_device(): return result.transpose(0, 2, 1, 3, 4).reshape(rhs.shape)  1.55 us

profile of v4, /device:TPU:1, one launch (start us, length us, event | category | flops | bytes accessed | tf_op | source)
XLA Modules:
  0.0 52.1 jit_solution(10912187025737163332)
XLA Ops:
  0.0 50.5 %shard_map.82 = bf16[6,4,16,128]{3,2,1,0:T(8,128)(2,1)} custom-call(s32[2,5]{1,0:T(2,128)} %bitcast.13, s32[1,6]{1,0:T(1,128)} %bitcast.14, bf16[6,2,4,8,128]{4,3,2,1,0:T(8,128)(2,1)} %bitcast.11, bf16[6,2,4,8,128]{4,3,2,1,0:T(8,128)(2,1)} %bitcast.12, bf16[6,2,128,128]{3,2,1,0:T(8,128)(2,1)} %diag_hbm.1, bf16[5,2,128,128]{3,2,1,0:T(8,128)(2,1)} %lower_hbm.1, ...), custom_call_target="tpu_custom_call" | custom-call | tf_op jit(solution)/shard_map/pallas_call | solution.py:650
  50.5 1.5 %copy_bitcast_fusion = bf16[6,2,32,128]{3,2,1,0:T(8,128)(2,1)} fusion(bf16[6,4,16,128]{3,2,1,0:T(8,128)(2,1)} %shard_map.82), kind=kLoop, calls=%fused_computation | loop fusion | bytes 196608 | tf_op jit(solution)/shard_map/reshape | solution.py:712

commit v5 on v4

--- a/solution.py
+++ b/solution.py
@@ -30,8 +30,8 @@
 
 
 def kernel(
-    parent,
-    live_count,
+    parent_hbm,
+    live_hbm,
     rhs,
     upd,
     diag_hbm,
@@ -39,6 +39,8 @@
     vinv_hbm,
     upper_hbm,
     out,
+    parent,
+    live_count,
     diag,
     lower,
     vinv,
@@ -122,15 +124,31 @@
     loads = [
         pltpu.make_async_copy(upd.at[0], upd_first, load_sem.at[0]),
         pltpu.make_async_copy(rhs.at[0], rhs_first, load_sem.at[1]),
-        pltpu.make_async_copy(diag_hbm, diag, load_sem.at[2]),
-        pltpu.make_async_copy(lower_hbm, lower, load_sem.at[3]),
+        pltpu.make_async_copy(diag_hbm.at[0], diag.at[0], load_sem.at[2]),
+        pltpu.make_async_copy(lower_hbm.at[0], lower.at[0], load_sem.at[3]),
         pltpu.make_async_copy(vinv_hbm, vinv, load_sem.at[4]),
         pltpu.make_async_copy(upper_hbm, upper, load_sem.at[5]),
         pltpu.make_async_copy(rhs.at[:, :, x], rhs_own, load_sem.at[6]),
         pltpu.make_async_copy(upd.at[:, :, x], upd_all.at[0], load_sem.at[7]),
+        pltpu.make_async_copy(
+            diag_hbm.at[pl.ds(1, LEVELS - 1)],
+            diag.at[pl.ds(1, LEVELS - 1)],
+            load_sem.at[8],
+        ),
+        pltpu.make_async_copy(
+            lower_hbm.at[pl.ds(1, LEVELS - 2)],
+            lower.at[pl.ds(1, LEVELS - 2)],
+            load_sem.at[9],
+        ),
     ]
-    for copy in loads:
+    ints = [
+        pltpu.make_async_copy(parent_hbm, parent, load_sem.at[10]),
+        pltpu.make_async_copy(live_hbm, live_count, load_sem.at[11]),
+    ]
+    for copy in ints + loads:
         copy.start()
+    for copy in ints:
+        copy.wait()
     for l in range(LEVELS - 1):
         for s in range(2):
             ids_own[0, 2 * l + s] = parent[s, l]
@@ -210,7 +228,7 @@
     for copy in rs:
         copy.start()
 
-    for k in range(4, 8):
+    for k in range(4, 10):
         loads[k].wait()
     partner = at((0, 0, 1), 2, 1)
     part = pl.ds(32 * x, 32)
@@ -546,16 +564,17 @@
         incoming = incoming + ins[3][k].astype(F32)
 
     fwd = dot(spread(bases - incoming, 8), mats(diag, 5)) * live_of(5)
-    sol[5] = (dot(spread(fwd, 8), mats(vinv, 5)) * live_of(5)).astype(BF16)
+    answer = (dot(spread(fwd, 8), mats(vinv, 5)) * live_of(5)).astype(BF16)
+    sol[5] = answer.reshape(2, 8, 128)
 
     def share(first, count):
         span = pl.ds(first, count)
         for k in (2, 1, 3):
             remote(
-                sol.at[span], out.at[span, x], send.at[9], recv.at[9], xs[k], g
+                sol.at[span], out.at[span, :, x], send.at[9], recv.at[9], xs[k], g
             ).start()
         pltpu.make_async_copy(
-            sol.at[span], out.at[span, x], own_sem.at[first]
+            sol.at[span], out.at[span, :, x], own_sem.at[first]
         ).start()
 
     chip = y * NZ + z
@@ -592,11 +611,15 @@
         else:
             ends = [lax.rem(parent[s, 4], 128) for s in range(2)]
         above = jnp.concatenate(
-            [half(top_tab[p // 4, lax.rem(p // 2, 2)], p) for p in ends], axis=0
+            [
+                top_tab[p // 4, lax.rem(p // 2, 2), lax.rem(p, 2)].astype(F32)
+                for p in ends
+            ],
+            axis=0,
         )
         low = dot(spread(above, 8), chain[k])
         value = fv[k] + low if k % 2 == 1 else fv[k] - low
-        sol[k] = (value * live_of(k)).astype(BF16)
+        sol[k] = (value * live_of(k)).astype(BF16).reshape(2, 8, 128)
     share(0, 5)
 
     wait(in0.at[pl.ds(1, 15)], send.at[0])
@@ -626,9 +649,9 @@
     for first, count in ((5, 1), (0, 5)):
         span = pl.ds(first, count)
         pltpu.make_async_copy(
-            sol.at[span], out.at[span, x], own_sem.at[first]
+            sol.at[span], out.at[span, :, x], own_sem.at[first]
         ).wait()
-    whole = out.at[:, pl.ds(0, NX - 1)]
+    whole = out.at[:, :, pl.ds(0, NX - 1)]
     wait(whole, send.at[9])
     wait(whole, recv.at[9])
 
@@ -638,7 +661,6 @@
         levels, slots, rows, width = rhs.shape
         part = rows // NX
         hbm = pl.BlockSpec(memory_space=pl.ANY)
-        smem = pl.BlockSpec(memory_space=pltpu.SMEM)
         dma = pltpu.SemaphoreType.DMA
         pair = slots * width
         tile = (slots * part, width)
@@ -649,10 +671,12 @@
 
         result = pl.pallas_call(
             kernel,
-            out_shape=jax.ShapeDtypeStruct((levels, NX) + tile, BF16),
-            in_specs=[smem, smem] + [hbm] * 6,
+            out_shape=pltpu.VMEM((levels,) + split, BF16),
+            in_specs=[hbm] * 8,
             out_specs=hbm,
             scratch_shapes=[
+                pltpu.SMEM(parent.shape[::-1], jnp.int32),
+                pltpu.SMEM(live_count.shape[::-1], jnp.int32),
                 vmem(*diag.shape),
                 vmem(*lower.shape),
                 vmem(*vinv.shape),
@@ -670,15 +694,15 @@
                 vmem(*split),
                 vmem(NX, levels, slots, part, width),
                 vmem(levels - 1, *tile, dtype=F32),
-                vmem(levels, *tile),
+                vmem(levels, slots, part, width),
                 vmem(levels - 1, pair, width),
                 vmem(sum(SIZES[1:4]) + 32, *tile),
                 vmem(NX, 4, *tile),
                 vmem(16, *tile),
                 [vmem(n, *tile) for n in (8, 16, 32, 32)],
                 vmem(2, *tile),
-                vmem(32, NC, *tile),
-                dma((8,)),
+                vmem(32, NC, slots, part, width),
+                dma((12,)),
                 dma((11,)),
                 dma((11,)),
                 dma((NX - 1,)),
@@ -708,8 +732,7 @@
             vinv,
             upper,
         )
-        result = result.reshape(levels, NX, slots, part, width)
-        return result.transpose(0, 2, 1, 3, 4).reshape(rhs.shape)
+        return result.reshape(rhs.shape)
 
     return jax.shard_map(
         on_device,

time: 52.3 us -> 50.4 us (0.964)
  local copies, waits for them, and re-layouts: 1.55 us -> 0.64 us
  Pallas kernels: 50.5 us -> 49.7 us
    reshape x1 -> x0, local copies, waits for them, and re-layouts: 1.55 us -> none  [on_device(): return result.transpose(0, 2, 1, 3, 4).reshape(rhs.shape)]
    pallas_call x1, Pallas kernels: 50.5 us -> 49.7 us  [on_device(): pl.pallas_call(kernel, out_shape=pltpu.VMEM((levels,) + split, BF16), in_...]
    unnamed x0 -> x1, local copies, waits for them, and re-layouts: none -> 0.64 us
where the time goes in v5:
time: 50.4 us
  Pallas kernels  49.7 us (99%)
  local copies, waits for them, and re-layouts  0.64 us (1%)
    pallas_call x1, Pallas kernels, on_device(): pl.pallas_call(kernel, out_shape=pltpu.VMEM((levels,) + split, BF16), in_...  49.7 us

profile of v5, /device:TPU:1, one launch (start us, length us, event | category | flops | bytes accessed | tf_op | source)
XLA Modules:
  0.0 50.4 jit_solution(4213990604945047384)
XLA Ops:
  0.0 49.7 %shard_map.82 = bf16[6,2,4,8,128]{4,3,2,1,0:T(8,128)(2,1)S(1)} custom-call(s32[2,5]{1,0:T(2,128)} %bitcast.8, s32[1,6]{1,0:T(1,128)} %bitcast.9, bf16[6,2,4,8,128]{4,3,2,1,0:T(8,128)(2,1)} %bitcast.6, bf16[6,2,4,8,128]{4,3,2,1,0:T(8,128)(2,1)} %bitcast.7, bf16[6,2,128,128]{3,2,1,0:T(8,128)(2,1)} %diag_hbm.1, bf16[5,2,128,128]{3,2,1,0:T(8,128)(2,1)} %lower_hbm.1, ...), custom_call_target="tpu_custom_call" | custom-call | tf_op jit(solution)/shard_map/pallas_call | solution.py:672
  49.7 0.6 %copy.10 = bf16[6,2,32,128]{3,2,1,0:T(8,128)(2,1)} copy(bf16[6,2,32,128]{3,2,1,0:T(8,128)(2,1)S(1)} %bitcast.5) | data formatting | bytes 196608

commit v6 on v5

--- a/solution.py
+++ b/solution.py
@@ -52,6 +52,7 @@
     picks,
     ftabs,
     ids_own,
+    ids_mate,
     ids,
     rhs_own,
     rhs_first,
@@ -66,6 +67,8 @@
     ins,
     mate,
     top_tab,
+    mate_send,
+    mate_recv,
     load_sem,
     send,
     recv,
@@ -378,9 +381,10 @@
             total = total - upd_all[k, l].astype(F32).reshape(16, 128)
         return total
 
+    remote(ids_own, ids_mate, send.at[5], recv.at[5], x, partner).start()
+    product(diag, lower, ml, 1)
     table_direct(1)
     table_ring(0)
-    product(diag, lower, ml, 1)
     for copy in rs:
         copy.wait_recv()
     bases = base(1)
@@ -389,20 +393,34 @@
     for k in range(1, 16):
         incoming = incoming + in0[k].astype(F32)
 
+    def mate_terms(l, sent):
+        i = 2 * (l - 3)
+        mate[i] = sent.astype(BF16)
+        remote(
+            mate.at[i], mate.at[i + 1], mate_send.at[l - 3], mate_recv.at[l - 3], x, partner
+        ).start()
+        wait(mate.at[i + 1], mate_recv.at[l - 3])
+        theirs = mate[i + 1].astype(F32)
+        return [
+            (ids_mate[0, 2 * l], theirs[:8]),
+            (ids_mate[0, 2 * l + 1], theirs[8:]),
+        ]
+
+    def masked(p, v, rel, n):
+        return jnp.where(target(p, n) == 2 * rel, twice(v), jnp.zeros((16, 128), F32))
+
     for l in (1, 2, 3):
         n, mz, my = SIZES[l], CHIPS_Z[l], CHIPS_Y[l]
         total = bases - incoming
         sent = dot(spread(total, 8), ml[l]) * live_of(l)
-        a, b = twice(sent[:8]), twice(sent[8:])
-        zero = jnp.zeros_like(a)
-        pa, pb = target(parent[0, l], n), target(parent[1, l], n)
+        terms = [(parent[0, l], sent[:8]), (parent[1, l], sent[8:])]
+        if l == 3:
+            terms += mate_terms(l, sent)
 
         def tile(rel):
-            return (
-                jnp.where(pa == 2 * rel, a, zero) + jnp.where(pb == 2 * rel, b, zero)
-            ).astype(BF16)
-
-        offs = offsets(mz, my, 2)
+            return sum(masked(p, v, rel, n) for p, v in terms).astype(BF16)
+
+        offs = offsets(mz, my, 1 if l == 3 else 2)
         goals = [at(o, mz, my) for o in offs]
         start = sum(SIZES[1:l])
         for k, goal in enumerate(goals):
@@ -422,6 +440,7 @@
             rows_swap(0)
             forward(0, base(0))
         if l == 2:
+            wait(ids_mate, recv.at[5])
             mine = lax.rem(g, 32)
             for s in range(10):
                 ids[mine, s] = ids_own[0, s]
@@ -442,15 +461,15 @@
                 wait(direct_view(j), tab_recv.at[0, j - 1])
                 core_swap(j)
         if l == 3:
-            ring_wait(2)
-            ring_wait(3)
-            rows_swap(2)
-            core_swap(3)
             wait(ids.at[pl.ds(0, 15)], recv.at[8])
             half_ids = ids.at[pl.ds(16 * up_row, 16)]
             remote(
                 half_ids, half_ids, send.at[7], recv.at[7], x, at((1, 0, 0), 8, 2)
             ).start()
+            ring_wait(2)
+            ring_wait(3)
+            rows_swap(2)
+            core_swap(3)
         product(diag, lower, ml, l + 1)
         product(upper, vinv, uv_own, l)
         if l == 3:
@@ -482,34 +501,21 @@
                         ]
             pick_share(0)
         bases = base(l + 1)
-        wait(ins[l - 1].at[pl.ds(0, n - 1)], recv.at[l])
+        wait(ins[l - 1].at[pl.ds(0, len(goals))], recv.at[l])
         incoming = own
-        for k in range(n - 1):
+        for k in range(len(goals)):
             incoming = incoming + ins[l - 1][k].astype(F32)
 
     total = bases - incoming
     sent = dot(spread(total, 8), ml[4]) * live_of(4)
-    mate[0] = sent.astype(BF16)
-    remote(mate.at[0], mate.at[1], send.at[5], recv.at[5], x, partner).start()
-    pa, pb = target(parent[0, 4], 64), target(parent[1, 4], 64)
-    other = lax.rem(partner, 32)
-    pc, pd = target(ids[other, 8], 64), target(ids[other, 9], 64)
+    terms = [(parent[0, 4], sent[:8]), (parent[1, 4], sent[8:])]
     offs = offsets(8, 4, 1)
     goals = [at(o, 8, 4) for o in offs]
-    a, b = twice(sent[:8]), twice(sent[8:])
     bases = base(5)
-    wait(mate.at[1], recv.at[5])
-    third = mate[1].astype(F32)
-    d, e = twice(third[:8]), twice(third[8:])
-    zero = jnp.zeros_like(a)
+    terms += mate_terms(4, sent)
 
     def tile4(goal):
-        return (
-            jnp.where(pa == 2 * goal, a, zero)
-            + jnp.where(pb == 2 * goal, b, zero)
-            + jnp.where(pc == 2 * goal, d, zero)
-            + jnp.where(pd == 2 * goal, e, zero)
-        ).astype(BF16)
+        return sum(masked(p, v, goal, 64) for p, v in terms).astype(BF16)
 
     start = sum(SIZES[1:4])
     for k, goal in enumerate(goals):
@@ -625,10 +631,12 @@
     wait(in0.at[pl.ds(1, 15)], send.at[0])
     for copy in rs:
         copy.wait_send()
-    for l in (1, 2, 3):
+    for l in (1, 2):
         wait(ins[l - 1].at[pl.ds(0, SIZES[l] - 1)], send.at[l])
-        if l < 3:
-            wait(direct_view(l), tab_send.at[0, l - 1])
+        wait(direct_view(l), tab_send.at[0, l - 1])
+    wait(ins[2].at[pl.ds(0, 15)], send.at[3])
+    for i in range(2):
+        wait(mate.at[2 * i], mate_send.at[i])
     for step in range(4):
         for i in range(2):
             wait(ring_view(i, step), ring_send.at[i, step])
@@ -641,7 +649,7 @@
     for i in range(2):
         wait(pick_view(i), pick_send.at[i])
     wait(ins[3].at[pl.ds(0, 31)], send.at[4])
-    wait(mate.at[0], send.at[5])
+    wait(ids_own, send.at[5])
     wait(top_tab.at[pl.ds(0, 31), 0], send.at[6])
     wait(half_ids, send.at[7])
     wait(ids.at[pl.ds(0, 15)], send.at[8])
@@ -688,6 +696,7 @@
                 [vmem(n, NX, width // NX, width) for n in (12, 8)],
                 [vmem(SIZES[l] // NC, NC, *tile) for l in range(4)],
                 pltpu.SMEM((1, 128), jnp.int32),
+                pltpu.SMEM((1, 128), jnp.int32),
                 pltpu.SMEM((32, 128), jnp.int32),
                 vmem(levels, slots, part, width),
                 vmem(*split),
@@ -699,9 +708,11 @@
                 vmem(sum(SIZES[1:4]) + 32, *tile),
                 vmem(NX, 4, *tile),
                 vmem(16, *tile),
-                [vmem(n, *tile) for n in (8, 16, 32, 32)],
-                vmem(2, *tile),
+                [vmem(n, *tile) for n in (8, 16, 16, 32)],
+                vmem(4, *tile),
                 vmem(32, NC, slots, part, width),
+                dma((2,)),
+                dma((2,)),
                 dma((12,)),
                 dma((11,)),
                 dma((11,)),

time: 50.4 us -> 49.1 us (0.974)
  Pallas kernels: 49.7 us -> 48.4 us
    pallas_call x1, Pallas kernels: 49.7 us -> 48.4 us  [on_device(): pl.pallas_call(kernel, out_shape=pltpu.VMEM((levels,) + split, BF16), in_...]
where the time goes in v6:
time: 49.1 us
  Pallas kernels  48.4 us (99%)
  local copies, waits for them, and re-layouts  0.64 us (1%)
    pallas_call x1, Pallas kernels, on_device(): pl.pallas_call(kernel, out_shape=pltpu.VMEM((levels,) + split, BF16), in_...  48.4 us

profile of v6, /device:TPU:1, one launch (start us, length us, event | category | flops | bytes accessed | tf_op | source)
XLA Modules:
  0.0 49.1 jit_solution(7489516640868164648)
XLA Ops:
  0.0 48.4 %shard_map.82 = bf16[6,2,4,8,128]{4,3,2,1,0:T(8,128)(2,1)S(1)} custom-call(s32[2,5]{1,0:T(2,128)} %bitcast.8, s32[1,6]{1,0:T(1,128)} %bitcast.9, bf16[6,2,4,8,128]{4,3,2,1,0:T(8,128)(2,1)} %bitcast.6, bf16[6,2,4,8,128]{4,3,2,1,0:T(8,128)(2,1)} %bitcast.7, bf16[6,2,128,128]{3,2,1,0:T(8,128)(2,1)} %diag_hbm.1, bf16[5,2,128,128]{3,2,1,0:T(8,128)(2,1)} %lower_hbm.1, ...), custom_call_target="tpu_custom_call" | custom-call | tf_op jit(solution)/shard_map/pallas_call | solution.py:680
  48.4 0.6 %copy.10 = bf16[6,2,32,128]{3,2,1,0:T(8,128)(2,1)} copy(bf16[6,2,32,128]{3,2,1,0:T(8,128)(2,1)S(1)} %bitcast.5) | data formatting | bytes 196608

commit v7 on v6

--- a/solution.py
+++ b/solution.py
@@ -46,6 +46,7 @@
     vinv,
     upper,
     ml,
+    top,
     uv_own,
     uv_part,
     tabs,
@@ -179,6 +180,18 @@
     def twice(v):
         return jnp.concatenate([v, v], axis=0)
 
+    def tiles(own, ref, places):
+        sums = [own]
+        for i, k in enumerate(places):
+            tile = ref[k].astype(F32)
+            if i < 3:
+                sums.append(tile)
+            else:
+                sums[i % 4] = sums[i % 4] + tile
+        while len(sums) > 1:
+            sums = [sum(sums[i : i + 2]) for i in range(0, len(sums), 2)]
+        return sums[0]
+
     def target(p, n):
         return lax.rem(p, 2 * n) - slotrow
 
@@ -389,9 +402,7 @@
         copy.wait_recv()
     bases = base(1)
     wait(in0.at[pl.ds(1, 15)], recv.at[0])
-    incoming = build0[x, 0].astype(F32)
-    for k in range(1, 16):
-        incoming = incoming + in0[k].astype(F32)
+    incoming = tiles(build0[x, 0].astype(F32), in0, range(1, 16))
 
     def mate_terms(l, sent):
         i = 2 * (l - 3)
@@ -502,9 +513,7 @@
             pick_share(0)
         bases = base(l + 1)
         wait(ins[l - 1].at[pl.ds(0, len(goals))], recv.at[l])
-        incoming = own
-        for k in range(len(goals)):
-            incoming = incoming + ins[l - 1][k].astype(F32)
+        incoming = tiles(own, ins[l - 1], range(len(goals)))
 
     total = bases - incoming
     sent = dot(spread(total, 8), ml[4]) * live_of(4)
@@ -534,6 +543,8 @@
     f_share(4)
     product(upper, vinv, uv_own, 4)
     product(upper, vinv, uv_own, 0)
+    for s in range(2):
+        top[pl.ds(128 * s, 128), :] = dot(diag[5, s], vinv[5, s]).astype(BF16)
     wait(core_view(4), tab_recv.at[1, 3])
     for k in range(4):
         for s in range(2):
@@ -565,12 +576,9 @@
             consts.append(const)
         fv[k] = jnp.concatenate(consts, axis=0)
     wait(ins[3].at[pl.ds(0, 31)], recv.at[4])
-    incoming = own
-    for k in range(31):
-        incoming = incoming + ins[3][k].astype(F32)
-
-    fwd = dot(spread(bases - incoming, 8), mats(diag, 5)) * live_of(5)
-    answer = (dot(spread(fwd, 8), mats(vinv, 5)) * live_of(5)).astype(BF16)
+    incoming = tiles(own, ins[3], range(31))
+
+    answer = (dot(spread(bases - incoming, 8), top[...]) * live_of(5)).astype(BF16)
     sol[5] = answer.reshape(2, 8, 128)
 
     def share(first, count):
@@ -690,6 +698,7 @@
                 vmem(*vinv.shape),
                 vmem(*upper.shape),
                 vmem(levels - 1, pair, width),
+                vmem(pair, width),
                 vmem(levels - 1, pair, width),
                 vmem(4, slots, width // NX, width),
                 [vmem(SIZES[l] // NC, NC, slots, width // NX, width) for l in range(4)],

time: 49.1 us -> 49 us (level)
  no operation moved by 1% of the time
where the time goes in v7:
time: 49 us; the launch traced here: 48.9 us
  Pallas kernels  48.3 us (99%)
  local copies, waits for them, and re-layouts  0.64 us (1%)
    pallas_call x1, Pallas kernels, on_device(): pl.pallas_call(kernel, out_shape=pltpu.VMEM((levels,) + split, BF16), in_...  48.3 us

profile of v7, /device:TPU:1, one launch (start us, length us, event | category | flops | bytes accessed | tf_op | source)
XLA Modules:
  0.0 48.9 jit_solution(6315587192880162413)
XLA Ops:
  0.0 48.3 %shard_map.82 = bf16[6,2,4,8,128]{4,3,2,1,0:T(8,128)(2,1)S(1)} custom-call(s32[2,5]{1,0:T(2,128)} %bitcast.8, s32[1,6]{1,0:T(1,128)} %bitcast.9, bf16[6,2,4,8,128]{4,3,2,1,0:T(8,128)(2,1)} %bitcast.6, bf16[6,2,4,8,128]{4,3,2,1,0:T(8,128)(2,1)} %bitcast.7, bf16[6,2,128,128]{3,2,1,0:T(8,128)(2,1)} %diag_hbm.1, bf16[5,2,128,128]{3,2,1,0:T(8,128)(2,1)} %lower_hbm.1, ...), custom_call_target="tpu_custom_call" | custom-call | tf_op jit(solution)/shard_map/pallas_call | solution.py:688
  48.3 0.6 %copy.10 = bf16[6,2,32,128]{3,2,1,0:T(8,128)(2,1)} copy(bf16[6,2,32,128]{3,2,1,0:T(8,128)(2,1)S(1)} %bitcast.5) | data formatting | bytes 196608
